TPU v7x, 32 devices: a whole 2x2x4 slice. The times are simulated.
32 devices in a mesh: spin: 2 (over core), band: 16 (over z, y, x).
Axes of the slice: x: 2, y: 2, z: 4, core: 2. Of those that a mesh axis runs over, the one named last changes fastest.
Arguments:
- orbitals: bfloat16 [128, 512000], P(('spin', 'band')), parts along dimension 0, may hold values from -40 to 40
Outputs:
- projector: float32 [32, 512000], P('spin', 'band'), parts along dimension 0
There are 2 independent parts, one for each index of `spin`. A program takes and returns all parts, laid end to end along the dimension named above; each array names one. Nothing has to cross between parts.
All inputs are finite; a program needn't handle non-finite values.
Results may differ from a plain program's by a relative error of at most 0.0003.
Values may be sent and summed in bfloat16 or wider, within the bound.
A program may use at most 512 MiB of HBM per device.

v0:
```python
import jax
import jax.numpy as jnp
from jax import lax
from jax.sharding import PartitionSpec as P

NG = 80
NP = 2


highest = lax.Precision.HIGHEST


def fourier_table(length):
    indices = jnp.arange(length, dtype=jnp.int32)
    nyquist = length // 2
    frequency = jnp.where(indices <= nyquist, indices, indices - nyquist)
    phases = frequency[:, None] * indices[None, :] % length
    angles = 2.0 * jnp.pi / length * phases.astype(jnp.float32)
    edges = (indices == 0) | (indices == nyquist)
    weights = jnp.where(edges, 1.0 / length, 2.0 / length).astype(jnp.float32)
    cosines = jnp.where((indices <= nyquist)[:, None], jnp.cos(angles), jnp.sin(angles))
    return (cosines * jnp.sqrt(weights)[:, None], frequency)


def screened_kernel(frequency, length):
    wavenumber = 2.0 * jnp.pi / length * frequency.astype(jnp.float32)
    squares = wavenumber * wavenumber
    totals = squares[:, None, None] + squares[None, :, None] + squares[None, None, :]
    return jnp.where(totals > 0.0, 1.0 / (0.0025 + totals), 0.0)


def coulomb(density, fourier, kernel):
    length = fourier.shape[0]
    values = density.reshape(length, length, length)
    for repeat in range(3):
        values = jnp.einsum("ka,abc->bck", fourier, values, precision=highest)
    values = values * kernel
    for repeat in range(3):
        values = jnp.einsum("ka,kbc->bca", fourier, values, precision=highest)
    return values.reshape(-1)


def body(orbitals):
    devices = lax.axis_size("band")
    owned_rows = orbitals.shape[0]
    points = orbitals.shape[1]
    stride = devices // NP
    fourier, frequency = fourier_table(NG)
    kernel = screened_kernel(frequency, NG)
    target = orbitals[0].astype(jnp.float32)
    empty = jnp.zeros((points,), jnp.float32)

    def exchange_term(partner):
        partner = partner.astype(jnp.float32)
        return -partner * coulomb(target * partner, fourier, kernel)

    chosen_rows = jnp.stack([orbitals[0], orbitals[owned_rows - 1]])
    slab_rows = lax.all_to_all(
        chosen_rows, "band", split_axis=1, concat_axis=0, tiled=True
    ).reshape(devices, 2, -1)
    target_slab = slab_rows[:, 0].astype(jnp.float32)
    partner_slab = slab_rows.reshape(NP, stride, 2, -1)[:, 0, 1]
    partners = lax.all_gather(partner_slab, "band", axis=1, tiled=True)

    def advance_local(number, vectors):
        return vectors + exchange_term(
            lax.dynamic_index_in_dim(partners, number, 0, keepdims=False)
        )

    vectors = lax.fori_loop(0, NP, advance_local, empty)
    vector_slab = lax.all_to_all(vectors[None, :], "band", split_axis=1, concat_axis=0, tiled=True)
    partial_intersection = (
        jnp.einsum("ap,bp->ab", target_slab, vector_slab, precision=highest) / NG**3
    )
    intersection = lax.psum(partial_intersection, "band")
    metric = -0.5 * (intersection + intersection.T)
    factor = jnp.linalg.cholesky(metric)
    return jax.scipy.linalg.solve_triangular(factor, vector_slab, lower=True)


def solution(mesh):
    placed = (P(("spin", "band"), None),)
    return jax.shard_map(
        body, mesh=mesh, in_specs=placed, out_specs=P("spin", "band"), check_vma=False
    )
```

profile of v0, /device:TPU:0, one launch (start us, length us, event | category | flops | bytes accessed | tf_op | source)
XLA Modules:
  0.0 461.8 jit_solution(17051832790062764220)
XLA Ops:
  6.5 8.1 %slice_convert_fusion = (f32[1,512000]{1,0:T(1,128)}, bf16[1,512000]{1,0:T(2,128)(2,1)S(1)}, bf16[1,512000]{1,0:T(2,128)(2,1)S(1)}) fusion(bf16[4,512000]{1,0:T(4,128)(2,1)} %param.3), kind=kLoop, calls=%fused_computation.78 | loop fusion | flops 512000 | bytes 6144000 | tf_op jit(solution)/shard_map/convert_element_type | solution.py:50
  14.6 4.7 %pad_maximum_fusion = bf16[2,512000]{1,0:T(2,128)(2,1)S(1)} fusion(bf16[1,512000]{1,0:T(2,128)(2,1)S(1)} %get-tuple-element.210, bf16[1,512000]{1,0:T(2,128)(2,1)S(1)} %get-tuple-element.211), kind=kLoop, calls=%fused_computation.49 | loop fusion | flops 4096000 | bytes 4096000 | tf_op jit(solution)/shard_map/stack | solution.py:57
  19.3 56.0 %all_to_all.32 = bf16[2,16,32000]{2,0,1:T(2,128)(2,1)S(1)} all-to-all(bf16[2,16,32000]{2,0,1:T(2,128)(2,1)S(1)} %bitcast.79), channel_id=1, replica_groups=mesh['spin'=2,'band'=16] {'band'}, dimensions={1} | all-to-all | bytes 4096000 | tf_op jit(solution)/shard_map/all_to_all | solution.py:58
  75.3 0.2 copy.57
  75.6 1.3 copy-done
  76.9 0.8 slice.30
  77.8 0.1 broadcast_add_fusion
  77.8 73.5 %all-gather.3.cloned.1.call-done = bf16[2,1,1,512000]{3,1,0,2:T(2,128)(2,1)} async-done(((bf16[2,1,1,32000]{3,1,0,2:T(2,128)(2,1)}), bf16[2,1,1,512000]{3,1,0,2:T(2,128)(2,1)}) %all-gather.3.cloned.1.call-update) | async-done | bytes 2048016 | tf_op jit(solution)/shard_map/all_gather | solution.py:63
  151.4 7.4 %copy.56 = bf16[2,1,1,512000]{3,0,1,2:T(2,128)(2,1)} copy(bf16[2,1,1,512000]{3,1,0,2:T(2,128)(2,1)} %all-gather.3.cloned.1.call-done) | data formatting | bytes 4096000
  158.8 195.1 %while.15 = (s32[]{:T(128)}, f32[512000]{0:T(1024)}, bf16[2,512000]{1,0:T(2,128)(2,1)}, f32[512000]{0:T(1024)}, s32[80]{0:T(128)S(1)}, /*index=5*/pred[80]{0:T(5...) while((s32[]{:T(128)}, f32[512000]{0:T(1024)}, ...), condition=%wide.region_1.2_spmd.clone.clone, body=%wide.region_0.1_spmd.clone.clone.sunk | while | flops 2955686400 | bytes 64542360 | solution.py:70
  159.0 25.1 %convert_reduce_fusion.2 = (f32[512000]{0:T(1024)S(1)}, f32[1,512000]{1,0:T(1,128)}) fusion(bf16[2,512000]{1,0:T(2,128)(2,1)} %get-tuple-element.299, s32[]{:T(128)} %get-tuple-element.286), kind=kLoop, calls=%fused_computation.12.clone.1 | loop fusion | flops 1024000 | bytes 5120004 | tf_op jit(solution)/shard_map/while/body/eval_jaxpr/convert_element_type | solution.py:54
  184.1 2.7 reshape.152
  186.8 4.2 reshape.151
  191.0 3.3 mul.481
  194.3 5.2 %copy.64 = f32[80,80,80]{0,1,2:T(8,128)} copy(f32[80,80,80]{2,1,0:T(8,128)S(1)} %mul.481) | data formatting | bytes 4096000 | tf_op jit(solution)/shard_map/while/body/eval_jaxpr/mul | solution.py:55
  199.5 10.3 %fusion.91 = f32[80,80,80]{0,2,1:T(8,128)S(1)} fusion(f32[80,80,80]{0,1,2:T(8,128)} %copy.64, f32[80]{0:T(128)S(1)} %get-tuple-element.303, s32[80]{0:T(128)S(1)} %get-tuple-element.301, pred[80]{0:T(512)(128)(4,1)S(1)} %get-tuple-element.302), kind=kOutput, calls=%fused_computation.24.clone.1 | convolution fusion | flops 491590400 | bytes 4096720 | tf_op jit(solution)/shard_map/while/body/eval_jaxpr/ka,abc->bck/dot_general | solution.py:36
  209.8 8.8 %fusion.92 = f32[80,80,80]{0,2,1:T(8,128)S(1)} fusion(f32[80,80,80]{0,2,1:T(8,128)S(1)} %fusion.91, f32[80]{0:T(128)S(1)} %get-tuple-element.303, s32[80]{0:T(128)S(1)} %get-tuple-element.301, pred[80]{0:T(512)(128)(4,1)S(1)} %get-tuple-element.302), kind=kOutput, calls=%fused_computation.7.clone.1 | convolution fusion | flops 491590400 | bytes 4096720 | tf_op jit(solution)/shard_map/while/body/eval_jaxpr/ka,abc->bck/dot_general | solution.py:36
  218.5 3.9 fusion.93
  222.4 5.9 %fusion.94 = f32[80,80,80]{2,1,0:T(8,128)S(1)} fusion(f32[80,80,80]{2,1,0:T(8,128)S(1)} %fusion.93, f32[80]{0:T(128)S(1)} %get-tuple-element.303, s32[80]{0:T(128)S(1)} %get-tuple-element.301, pred[80]{0:T(512)(128)(4,1)S(1)} %get-tuple-element.302), kind=kOutput, calls=%fused_computation.9.clone.1 | convolution fusion | flops 491590400 | bytes 4096720 | tf_op jit(solution)/shard_map/while/body/eval_jaxpr/ka,kbc->bca/dot_general | solution.py:39
  228.3 5.1 %copy.65 = f32[80,80,80]{0,1,2:T(8,128)} copy(f32[80,80,80]{2,1,0:T(8,128)S(1)} %fusion.94) | data formatting | bytes 4096000 | tf_op jit(solution)/shard_map/while/body/eval_jaxpr/ka,kbc->bca/dot_general | solution.py:39
  233.4 10.4 %fusion.95 = f32[80,80,80]{0,2,1:T(8,128)S(1)} fusion(f32[80,80,80]{0,1,2:T(8,128)} %copy.65, f32[80]{0:T(128)S(1)} %get-tuple-element.303, s32[80]{0:T(128)S(1)} %get-tuple-element.301, pred[80]{0:T(512)(128)(4,1)S(1)} %get-tuple-element.302), kind=kOutput, calls=%fused_computation.19.clone.1 | convolution fusion | flops 491590400 | bytes 4096720 | tf_op jit(solution)/shard_map/while/body/eval_jaxpr/ka,kbc->bca/dot_general | solution.py:39
  243.8 2.9 fusion.96
  246.7 3.8 reshape.153
  250.6 3.8 select_add_fusion.2
  254.6 25.1 %convert_reduce_fusion.2 = (f32[512000]{0:T(1024)S(1)}, f32[1,512000]{1,0:T(1,128)}) fusion(bf16[2,512000]{1,0:T(2,128)(2,1)} %get-tuple-element.299, s32[]{:T(128)} %get-tuple-element.286), kind=kLoop, calls=%fused_computation.12.clone.1 | loop fusion | flops 1024000 | bytes 5120004 | tf_op jit(solution)/shard_map/while/body/eval_jaxpr/convert_element_type | solution.py:54
  279.7 2.7 reshape.152
  282.4 4.2 reshape.151
  286.6 3.3 mul.481
  289.9 5.3 %copy.64 = f32[80,80,80]{0,1,2:T(8,128)} copy(f32[80,80,80]{2,1,0:T(8,128)S(1)} %mul.481) | data formatting | bytes 4096000 | tf_op jit(solution)/shard_map/while/body/eval_jaxpr/mul | solution.py:55
  295.2 10.3 %fusion.91 = f32[80,80,80]{0,2,1:T(8,128)S(1)} fusion(f32[80,80,80]{0,1,2:T(8,128)} %copy.64, f32[80]{0:T(128)S(1)} %get-tuple-element.303, s32[80]{0:T(128)S(1)} %get-tuple-element.301, pred[80]{0:T(512)(128)(4,1)S(1)} %get-tuple-element.302), kind=kOutput, calls=%fused_computation.24.clone.1 | convolution fusion | flops 491590400 | bytes 4096720 | tf_op jit(solution)/shard_map/while/body/eval_jaxpr/ka,abc->bck/dot_general | solution.py:36
  305.5 8.8 %fusion.92 = f32[80,80,80]{0,2,1:T(8,128)S(1)} fusion(f32[80,80,80]{0,2,1:T(8,128)S(1)} %fusion.91, f32[80]{0:T(128)S(1)} %get-tuple-element.303, s32[80]{0:T(128)S(1)} %get-tuple-element.301, pred[80]{0:T(512)(128)(4,1)S(1)} %get-tuple-element.302), kind=kOutput, calls=%fused_computation.7.clone.1 | convolution fusion | flops 491590400 | bytes 4096720 | tf_op jit(solution)/shard_map/while/body/eval_jaxpr/ka,abc->bck/dot_general | solution.py:36
  314.3 3.6 fusion.93
  317.8 5.9 %fusion.94 = f32[80,80,80]{2,1,0:T(8,128)S(1)} fusion(f32[80,80,80]{2,1,0:T(8,128)S(1)} %fusion.93, f32[80]{0:T(128)S(1)} %get-tuple-element.303, s32[80]{0:T(128)S(1)} %get-tuple-element.301, pred[80]{0:T(512)(128)(4,1)S(1)} %get-tuple-element.302), kind=kOutput, calls=%fused_computation.9.clone.1 | convolution fusion | flops 491590400 | bytes 4096720 | tf_op jit(solution)/shard_map/while/body/eval_jaxpr/ka,kbc->bca/dot_general | solution.py:39
  323.8 5.1 %copy.65 = f32[80,80,80]{0,1,2:T(8,128)} copy(f32[80,80,80]{2,1,0:T(8,128)S(1)} %fusion.94) | data formatting | bytes 4096000 | tf_op jit(solution)/shard_map/while/body/eval_jaxpr/ka,kbc->bca/dot_general | solution.py:39
  328.9 10.4 %fusion.95 = f32[80,80,80]{0,2,1:T(8,128)S(1)} fusion(f32[80,80,80]{0,1,2:T(8,128)} %copy.65, f32[80]{0:T(128)S(1)} %get-tuple-element.303, s32[80]{0:T(128)S(1)} %get-tuple-element.301, pred[80]{0:T(512)(128)(4,1)S(1)} %get-tuple-element.302), kind=kOutput, calls=%fused_computation.19.clone.1 | convolution fusion | flops 491590400 | bytes 4096720 | tf_op jit(solution)/shard_map/while/body/eval_jaxpr/ka,kbc->bca/dot_general | solution.py:39
  339.3 2.9 fusion.96
  342.2 3.8 reshape.153
  346.1 4.4 select_add_fusion.2
  353.9 52.2 %all_to_all.33 = f32[1,16,32000]{2,0,1:T(1,128)S(1)} all-to-all(f32[1,16,32000]{2,0,1:T(1,128)} %bitcast.78), channel_id=1, replica_groups=mesh['spin'=2,'band'=16] {'band'}, dimensions={1} | all-to-all | bytes 4096000 | tf_op jit(solution)/shard_map/all_to_all | solution.py:71
  406.1 1.5 fusion.49
  407.6 39.5 %psum.7 = f32[16,16]{1,0:T(8,128)S(1)} all-reduce(f32[16,16]{1,0:T(8,128)S(1)} %fusion.49), channel_id=1, replica_groups=mesh['spin'=2,'band'=16] {'band'}, use_global_device_ids=true, to_apply=%region_2.3 | all-reduce | flops 256 | bytes 2048 | tf_op jit(solution)/shard_map/psum | solution.py:75
  447.1 0.1 copy.29
  447.2 0.1 copy.30
  447.2 1.5 cholesky.16
  448.7 0.6 compare_reduce_fusion
  449.4 0.6 fusion.52
  450.0 1.2 custom-call.7
  451.3 3.2 fusion.43
  (12 shorter events, 0.1 us)
Async XLA Ops:
  6.5 144.8 %all-gather.3.cloned.1.call-start = ((), (), s32[]{:S(2)}) async-start(), calls=%async_computation.2 | async-start | bytes 4352000 | tf_op jit(solution)/shard_map/all_gather | solution.py:63
  75.5 1.3 copy-start
  353.9 52.2 %copy-start.1 = (bf16[2,16,32000]{2,1,0:T(8,128)(2,1)S(1)}, bf16[2,16,32000]{2,1,0:T(8,128)(2,1)}, u32[]{:S(2)}) copy-start(bf16[2,16,32000]{2,1,0:T(8,128)(2,1)} %copy-done) | copy-start | bytes 6144004
Sparse Core Ops, SparseCore 0:
  77.8 73.4 all-gather.2
where the time goes:
time: 466 us; the launch traced here: 462 us
  blocking collectives  148 us (32%)
  matrix products  88.6 us (19%)
  other arithmetic  82 us (18%)
  waiting for transfers between devices  73.5 us (16%)
  local copies, waits for them, and re-layouts  52.1 us (11%)
  between operations  14 us (3%)
    all_gather x1, waiting for transfers between devices, body(): partners = lax.all_gather(partner_slab, 'band', axis=1, tiled=True)  73.5 us
    all_to_all x1, blocking collectives, body(): lax.all_to_all(chosen_rows, 'band', split_axis=1, concat_axis=0, tiled=True)  56 us
    all_to_all x1, blocking collectives, body(): lax.all_to_all(vectors[None, :], 'band', split_axis=1, concat_axis=0, til...  52.2 us
    convert_element_type x2, other arithmetic, exchange_term(): partner = partner.astype(jnp.float32)  50.2 us
    dot_general x6, matrix products, coulomb(): values = jnp.einsum('ka,abc->bck', fourier, values, precision=highest)  45.5 us
    psum x1, blocking collectives, body(): intersection = lax.psum(partial_intersection, 'band')  39.5 us
    dot_general x6, matrix products, coulomb(): values = jnp.einsum('ka,kbc->bca', fourier, values, precision=highest)  38.4 us
    mul x2, local copies, waits for them, and re-layouts, exchange_term(): return -partner * coulomb(target * partner, fourier, kernel)  10.5 us
  transfers between devices with their start and end apart: 1, of which 1 were waited for; matrix products, arithmetic and copies ran while one was open for 0% of the time, Pallas kernels for 0%

commit v1 on v0

v1 whole, which is shorter than its diff:
```python
import functools

import jax
import jax.numpy as jnp
import numpy as np
from jax import lax
from jax.experimental import pallas as pl
from jax.experimental.pallas import tpu as pltpu
from jax.sharding import PartitionSpec as P

NG = 80
NP = 2
PAD = 128
QUARTERS = 4
highest = lax.Precision.HIGHEST


def tables(length):
    indices = np.arange(length)
    nyquist = length // 2
    frequency = np.where(indices <= nyquist, indices, indices - nyquist)
    angles = 2.0 * np.pi / length * (frequency[:, None] * indices[None, :] % length)
    edges = (indices == 0) | (indices == nyquist)
    weights = np.where(edges, 1.0 / length, 2.0 / length)
    fourier = np.where((indices <= nyquist)[:, None], np.cos(angles), np.sin(angles))
    fourier = (fourier * np.sqrt(weights)[:, None]).astype(np.float32)
    squares = ((2.0 * np.pi / length * frequency) ** 2).astype(np.float32)
    return fourier, squares


def halves(table):
    high = table.astype(jnp.bfloat16)
    low = (table - high.astype(np.float32)).astype(jnp.bfloat16)
    return high, low


def left_table(table):
    high, low = halves(table)
    return np.concatenate([high, high, low], axis=1)


def right_table(table, depth):
    high, low = halves(table)
    result = np.zeros((depth, 2 * PAD), dtype=high.dtype)
    result[: table.shape[0], : table.shape[1]] = high
    result[: table.shape[0], PAD : PAD + table.shape[1]] = low
    return result


def barrier_all(me, count):
    barrier = pltpu.get_barrier_semaphore()
    for step in range(1, count):
        pl.semaphore_signal(
            barrier, inc=1, device_id={"band": lax.rem(me + step, count)},
            device_id_type=pl.DeviceIdType.MESH,
        )
    pl.semaphore_wait(barrier, count - 1)


def remote(source, target, send, receive, device):
    return pltpu.make_async_remote_copy(
        src_ref=source, dst_ref=target, send_sem=send, recv_sem=receive,
        device_id={"band": device}, device_id_type=pl.DeviceIdType.MESH,
    )


def share_kernel(count, row, slabs, partners, gathered, first_send, column_send, plane_send,
                 receive, own_sem, slab_send, slab_receive, slab_own):
    me = lax.axis_index("band")
    planes = count // QUARTERS
    stride = count // NP
    column = lax.rem(me, QUARTERS)
    plane = lax.div(me, QUARTERS)
    base = plane * QUARTERS
    barrier_all(me, count)

    def first(r, q):
        return remote(row.at[q], partners.at[r, q], first_send.at[r, q - 1],
                      receive.at[r, q], lax.rem(me + q, count))

    def down(r, step):
        other = lax.rem(me + step * QUARTERS, count)
        return remote(partners.at[r, column], partners.at[r, column],
                      column_send.at[r, step - 1], receive.at[r, column], other)

    def across(r, step):
        other = base + lax.rem(column + step, QUARTERS)
        return remote(partners.at[r, column], partners.at[r, column],
                      plane_send.at[r, step - 1], receive.at[r, column], other)

    def slab(step):
        other = lax.rem(me + step, count)
        return remote(slabs.at[other], gathered.at[me], slab_send.at[step - 1],
                      slab_receive.at[step - 1], other)

    def arrived(r, q):
        remote(partners.at[r, q], partners.at[r, q], plane_send.at[r, 0],
               receive.at[r, q], me).wait_recv()

    for r in range(NP):
        @pl.when(me == r * stride)
        def _():
            for q in range(1, QUARTERS):
                first(r, q).start()
            own = pltpu.make_async_copy(row.at[0], partners.at[r, 0], own_sem)
            own.start()
            own.wait()

    for r in range(NP):
        @pl.when(me != r * stride)
        def _():
            arrived(r, column)

        @pl.when(plane == r * stride // QUARTERS)
        def _():
            for step in range(1, planes):
                down(r, step).start()

        for step in range(1, QUARTERS):
            across(r, step).start()

    mine = pltpu.make_async_copy(slabs.at[me], gathered.at[me], slab_own)
    mine.start()
    for step in range(1, count):
        slab(step).start()

    for r in range(NP):
        for step in range(1, QUARTERS):
            arrived(r, lax.rem(column + step, QUARTERS))
    for r in range(NP):
        @pl.when(me == r * stride)
        def _():
            for q in range(1, QUARTERS):
                first(r, q).wait_send()

        @pl.when(plane == r * stride // QUARTERS)
        def _():
            for step in range(1, planes):
                down(r, step).wait_send()

        for step in range(1, QUARTERS):
            across(r, step).wait_send()
    mine.wait()
    for step in range(1, count):
        slab(step).wait()


def share(row, slabs, count):
    planes = count // QUARTERS
    anywhere = pl.BlockSpec(memory_space=pl.ANY)
    dma = pltpu.SemaphoreType.DMA
    return pl.pallas_call(
        functools.partial(share_kernel, count),
        out_shape=(
            jax.ShapeDtypeStruct((NP,) + row.shape, row.dtype),
            jax.ShapeDtypeStruct(slabs.shape, slabs.dtype),
        ),
        in_specs=[anywhere] * 2,
        out_specs=(anywhere, anywhere),
        scratch_shapes=[
            dma((NP, QUARTERS - 1)), dma((NP, planes - 1)), dma((NP, QUARTERS - 1)),
            dma((NP, QUARTERS)), dma, dma((count - 1,)), dma((count - 1,)), dma,
        ],
        compiler_params=pltpu.CompilerParams(
            collective_id=0, has_side_effects=True, vmem_limit_bytes=1 << 20
        ),
        name="share",
    )(row, slabs)


def sum_kernel(count, part, total, held, send, receive):
    me = lax.axis_index("band")
    barrier_all(me, count)

    def copy(step):
        return remote(part, held.at[step], send.at[step], receive.at[step],
                      lax.rem(me + step, count))

    for step in range(1, count):
        copy(step).start()
    held[0] = part[...]
    for step in range(1, count):
        copy(step).wait()
    total[...] = jnp.sum(held[...], axis=0)


def sum_all(part, count):
    rows, columns = part.shape
    width = -(-columns // PAD) * PAD
    padded = jnp.pad(part, ((0, 0), (0, width - columns)))
    vmem = pl.BlockSpec(memory_space=pltpu.VMEM)
    total = pl.pallas_call(
        functools.partial(sum_kernel, count),
        out_shape=jax.ShapeDtypeStruct((rows, width), jnp.float32),
        in_specs=[vmem],
        out_specs=vmem,
        scratch_shapes=[
            pltpu.VMEM((count, rows, width), jnp.float32),
            pltpu.SemaphoreType.DMA((count,)),
            pltpu.SemaphoreType.DMA((count,)),
        ],
        compiler_params=pltpu.CompilerParams(collective_id=1, has_side_effects=True),
        name="sum_all",
    )(padded)
    return total[:, :columns]


def split(values):
    high = values.astype(jnp.bfloat16)
    low = (values - high.astype(jnp.float32)).astype(jnp.bfloat16)
    return high, low


def dot(left, right):
    return lax.dot_general(left, right, (((1,), (0,)), ((), ())),
                           preferred_element_type=jnp.float32)


def from_left(table, values):
    high, low = split(values)
    return dot(table, jnp.concatenate([high, low, high], axis=0))


def from_right(values, table):
    high, low = split(values)
    both = dot(high, table)
    return both[:, :PAD] + both[:, PAD:] + dot(low, table[:, :PAD])


def exchange_kernel(target, partners, forward_left, inverse_left, forward_right, inverse_right,
                    row_squares, lane_squares, vectors, one, two):
    group = 8

    def ahead(step, carry):
        planes = pl.ds(step * group, group)
        left = target[planes].astype(jnp.float32)
        parts = []
        for r in range(NP):
            density = left * partners[r, planes].astype(jnp.float32)
            parts.append(from_right(density.reshape(group * NG, NG), forward_right[...]))
        values = jnp.concatenate(parts, axis=1).reshape(group, NG, NP * PAD)
        out = jnp.stack([from_left(forward_left[...], values[i]) for i in range(group)])
        one[:, pl.ds(pl.multiple_of(step * group, group), group), :] = jnp.swapaxes(out, 0, 1)
        return carry

    lax.fori_loop(0, NG // group, ahead, 0)

    def middle(step, carry):
        outs = []
        for i in range(group):
            number = step * group + i
            folded = jnp.where(number <= NG // 2, number, number - NG // 2)
            wave = (2.0 * np.pi / NG) * folded.astype(jnp.float32)
            totals = row_squares[...] + lane_squares[...] + wave * wave
            weight = jnp.where(totals > 0.0, 1.0 / (0.0025 + totals), 0.0)
            spectrum = from_left(forward_left[...], one[number]) * weight
            outs.append(from_left(inverse_left[...], spectrum))
        out = jnp.stack(outs)
        two[:, pl.ds(pl.multiple_of(step * group, group), group), :] = jnp.swapaxes(out, 0, 1)
        return carry

    lax.fori_loop(0, NG // group, middle, 0)

    def back(step, carry):
        planes = pl.ds(step * group, group)
        values = jnp.stack(
            [from_left(inverse_left[...], two[step * group + i]) for i in range(group)]
        ).reshape(group * NG, NP * PAD)
        total = jnp.zeros((group, NG, NG), jnp.float32)
        for r in range(NP):
            potential = from_right(values[:, r * PAD : (r + 1) * PAD], inverse_right[...])
            potential = potential.reshape(group, NG, PAD)[:, :, :NG]
            total -= partners[r, planes].astype(jnp.float32) * potential
        vectors[planes] = total
        return carry

    lax.fori_loop(0, NG // group, back, 0)


def exchange(target, partners):
    fourier, squares = tables(NG)
    lanes = np.zeros((PAD,), np.float32)
    lanes[:NG] = squares
    vmem = pl.BlockSpec(memory_space=pltpu.VMEM)
    return pl.pallas_call(
        exchange_kernel,
        out_shape=jax.ShapeDtypeStruct((NG, NG, NG), jnp.float32),
        in_specs=[vmem] * 8,
        out_specs=vmem,
        scratch_shapes=[pltpu.VMEM((NG, NG, NP * PAD), jnp.float32)] * 2,
        compiler_params=pltpu.CompilerParams(vmem_limit_bytes=48 << 20),
        cost_estimate=pl.CostEstimate(
            flops=12 * NP * NG**4, bytes_accessed=8 << 20, transcendentals=0
        ),
        name="exchange",
    )(
        target,
        partners,
        left_table(fourier),
        left_table(fourier.T.copy()),
        right_table(fourier.T.copy(), NG),
        right_table(fourier, PAD),
        np.broadcast_to(squares[:, None], (NG, NP * PAD)).copy(),
        np.tile(lanes, NP)[None, :],
    )


def body(orbitals):
    devices = lax.axis_size("band")
    owned_rows = orbitals.shape[0]
    points = orbitals.shape[1]
    target = orbitals[0]
    row = orbitals[owned_rows - 1].reshape(QUARTERS, points // QUARTERS // PAD, PAD)
    slabs = target.reshape(devices, 8, points // devices // 8)
    partners, target_slab = share(row, slabs, devices)
    vectors = exchange(target.reshape(NG, NG, NG), partners.reshape(NP, NG, NG, NG))
    vector_slab = lax.all_to_all(
        vectors.reshape(1, points), "band", split_axis=1, concat_axis=0, tiled=True
    )
    target_slab = target_slab.reshape(devices, points // devices).astype(jnp.float32)
    part = jnp.einsum("ap,bp->ab", target_slab, vector_slab, precision=highest) / NG**3
    intersection = sum_all(part, devices)
    metric = -0.5 * (intersection + intersection.T)
    factor = jnp.linalg.cholesky(metric)
    return jax.scipy.linalg.solve_triangular(factor, vector_slab, lower=True)


def solution(mesh):
    placed = (P(("spin", "band"), None),)
    return jax.shard_map(
        body, mesh=mesh, in_specs=placed, out_specs=P("spin", "band"), check_vma=False
    )
```

time: 466 us -> 205 us (0.44)
  blocking collectives: 148 us -> 0 us
  Pallas kernels: 0 us -> 99.7 us
  matrix products: 88.6 us -> 5.85 us
  other arithmetic: 82 us -> 4.71 us
  waiting for transfers between devices: 73.5 us -> 35.8 us
  between operations: 14 us -> 0.14 us
  starting transfers between devices: 0.01 us -> 11 us
  local copies, waits for them, and re-layouts: 52.1 us -> 46.8 us
    all_to_all x2 -> x0, blocking collectives: 108 us -> none  [the longest x1 56 us: body(): lax.all_to_all(chosen_rows, 'band', split_axis=1, concat_axis=0, tiled=True)]
    pallas_call x0 -> x3, Pallas kernels: none -> 99.7 us  [the longest x1 64.1 us: share(): pl.pallas_call(functools.partial(share_kernel, count), out_shape=(jax.Sha...]
    dot_general x12 -> x0, matrix products: 84 us -> none  [the longest x6 45.5 us: coulomb(): values = jnp.einsum('ka,abc->bck', fourier, values, precision=highest)]
    all_gather x1 -> x0, waiting for transfers between devices: 73.5 us -> none  [body(): partners = lax.all_gather(partner_slab, 'band', axis=1, tiled=True)]
    convert_element_type x3 -> x0, other arithmetic: 58.3 us -> none  [the longest x2 50.2 us: exchange_term(): partner = partner.astype(jnp.float32)]
    psum x1 -> x0, blocking collectives: 39.5 us -> none  [body(): intersection = lax.psum(partial_intersection, 'band')]
    all_to_all x0 -> x1, waiting for transfers between devices: none -> 35.8 us  [body(): lax.all_to_all(vectors.reshape(1, points), 'band', split_axis=1, concat_a...]
    slice x1 -> x2, local copies, waits for them, and re-layouts: 0.82 us -> 24.4 us  [the longest x1 23.6 us: body(): orbitals[owned_rows - 1].reshape(QUARTERS, points // QUARTERS // PAD, PAD)]
  transfers between devices with their start and end apart: 1 -> 1, of which waited for: 1 -> 1; matrix products, arithmetic and copies ran while one was open for 0% -> 1% of each run, Pallas kernels for 0% -> 0%
where the time goes in v1:
time: 205 us; the launch traced here: 204 us
  Pallas kernels  99.7 us (49%)
  local copies, waits for them, and re-layouts  46.8 us (23%)
  waiting for transfers between devices  35.8 us (17%)
  starting transfers between devices  11 us (5%)
  matrix products  5.85 us (3%)
  other arithmetic  4.71 us (2%)
    pallas_call x1, Pallas kernels, share(): pl.pallas_call(functools.partial(share_kernel, count), out_shape=(jax.Sha...  64.1 us
    all_to_all x1, waiting for transfers between devices, body(): lax.all_to_all(vectors.reshape(1, points), 'band', split_axis=1, concat_a...  35.8 us
    slice x1, local copies, waits for them, and re-layouts, body(): orbitals[owned_rows - 1].reshape(QUARTERS, points // QUARTERS // PAD, PAD)  23.6 us
    pallas_call x1, Pallas kernels, exchange(): pl.pallas_call(exchange_kernel, out_shape=jax.ShapeDtypeStruct((NG, NG, N...  21.4 us
    pallas_call x1, Pallas kernels, sum_all(): pl.pallas_call(functools.partial(sum_kernel, count), out_shape=jax.ShapeD...  14.2 us
    all_to_all x1, starting transfers between devices, body(): lax.all_to_all(vectors.reshape(1, points), 'band', split_axis=1, concat_a...  11 us
    reshape x1, local copies, waits for them, and re-layouts, body(): partners.reshape(NP, NG, NG, NG)  6.44 us
    all_to_all x1, local copies, waits for them, and re-layouts, body(): lax.all_to_all(vectors.reshape(1, points), 'band', split_axis=1, concat_a...  4.83 us
  transfers between devices with their start and end apart: 1, of which 1 were waited for; matrix products, arithmetic and copies ran while one was open for 1% of the time, Pallas kernels for 0%

profile of v1, /device:TPU:0, one launch (start us, length us, event | category | flops | bytes accessed | tf_op | source)
XLA Modules:
  0.0 204.1 jit_solution(16225225993893478088)
XLA Ops:
  0.0 23.6 %slice_reduce_fusion.1 = (bf16[512000]{0:T(1024)(128)(2,1)S(1)}, bf16[512000]{0:T(1024)(128)(2,1)S(1)}) fusion(bf16[4,512000]{1,0:T(4,128)(2,1)} %param.7), kind=kLoop, calls=%fused_computation.5 | loop fusion | bytes 4096000 | tf_op jit(solution)/shard_map/slice | solution.py:313
  23.6 1.5 reshape_squeeze.10.slabs
  25.1 2.6 %reshape_squeeze.11.target = bf16[80,80,80]{2,1,0:T(8,128)(2,1)} reshape(bf16[512000]{0:T(1024)(128)(2,1)S(1)} %get-tuple-element.10) | data formatting | bytes 2048000 | tf_op jit(solution)/shard_map/reshape;squeeze | solution.py:316
  27.8 64.1 %share.1 = (bf16[2,4,1000,128]{3,2,1,0:T(8,128)(2,1)S(1)}, bf16[16,8,4000]{2,1,0:T(8,128)(2,1)S(1)}) custom-call(bf16[4,1000,128]{2,1,0:T(8,128)(2,1)S(1)} %bitcast.25, bf16[16,8,4000]{2,1,0:T(8,128)(2,1)S(1)} %reshape_squeeze.10.slabs), custom_call_target="tpu_custom_call" | custom-call | tf_op jit(solution)/shard_map/share/pallas_call | solution.py:152
  91.8 0.0 copy-start.1
  91.8 1.3 copy-done.1
  93.1 0.0 copy-start.2
  93.1 1.0 copy-done.2
  94.1 0.0 copy-start.4
  94.1 0.0 copy-start.5
  94.1 0.0 copy-start.6
  94.2 0.0 copy-start.7
  94.2 0.0 copy-start.8
  94.2 0.0 copy-start.9
  94.2 6.4 %reshape.25.partners = bf16[2,80,80,80]{3,2,1,0:T(8,128)(2,1)} reshape(bf16[2,4,1000,128]{3,2,1,0:T(8,128)(2,1)} %copy-done.1) | data formatting | bytes 4096000 | tf_op jit(solution)/shard_map/reshape | solution.py:316
  100.6 0.0 copy-done.4
  100.6 0.0 copy-done.5
  100.6 0.0 copy-done.6
  100.6 0.0 copy-done.7
  100.6 0.0 copy-done.8
  100.7 0.0 copy-done.9
  100.7 0.0 copy-start
  100.7 1.4 copy-done
  102.1 21.4 %exchange.1 = f32[80,80,80]{2,1,0:T(8,128)S(1)} custom-call(bf16[80,80,80]{2,1,0:T(8,128)(2,1)S(1)} %copy-done, bf16[2,80,80,80]{3,2,1,0:T(8,128)(2,1)} %reshape.25.partners, bf16[80,240]{1,0:T(8,128)(2,1)S(1)} %copy-done.8, bf16[80,240]{1,0:T(8,128)(2,1)S(1)} %copy-done.7, bf16[80,256]{1,0:T(8,128)(2,1)S(1)} %copy-done.6, bf16[128,256]{1,0:T(8,128)(2,1)S(1)} %copy-done.5, ...), custom_call_target="tpu_custom_call" | custom-call | flops 983040000 | bytes 8388608 | tf_op jit(solution)/shard_map/exchange/pallas_call | solution.py:285
  123.5 4.8 %all_to_all.15 = f32[1,16,32000]{2,0,1:T(1,128)} reshape(f32[80,80,80]{2,1,0:T(8,128)S(1)} %exchange.1) | data formatting | bytes 4096000 | tf_op jit(solution)/shard_map/all_to_all | solution.py:317
  128.3 0.0 copy-start.3
  128.3 11.0 %all-to-all-start = ((f32[1,16,32000]{2,0,1:T(1,128)}), f32[1,16,32000]{2,0,1:T(1,128)S(1)}, u32[]{:S(2)}, u32[]{:S(2)}) async-start(f32[1,16,32000]{2,0,1:T(1,128)} %all_to_all.15), calls=%async_computation | async-start | bytes 4096000 | tf_op jit(solution)/shard_map/all_to_all | solution.py:317
  139.4 0.0 copy-done.3
  139.4 2.6 %reshape.24 = bf16[16,32000]{1,0:T(8,128)(2,1)} reshape(bf16[16,8,4000]{2,1,0:T(8,128)(2,1)S(1)} %copy-done.3) | data formatting | bytes 2048000 | tf_op jit(solution)/shard_map/reshape | solution.py:320
  142.0 35.8 %all-to-all-done = f32[1,16,32000]{2,0,1:T(1,128)S(1)} async-done(((f32[1,16,32000]{2,0,1:T(1,128)}), f32[1,16,32000]{2,0,1:T(1,128)S(1)}, u32[]{:S(2)}, u32[]{:S(2)}) %all-to-all-start) | async-done | bytes 2048032 | tf_op jit(solution)/shard_map/all_to_all | solution.py:317
  177.8 2.7 %fusion.6 = f32[16,16]{1,0:T(8,128)S(1)} fusion(bf16[16,32000]{1,0:T(8,128)(2,1)} %reshape.24, f32[1,16,32000]{2,0,1:T(1,128)S(1)} %all-to-all-done), kind=kOutput, calls=%fused_computation.8 | convolution fusion | flops 98304256 | bytes 3073024 | tf_op jit(solution)/shard_map/ap,bp->ab/dot_general | solution.py:321
  180.5 0.6 pad.4.part
  181.1 14.2 %sum_all.1 = f32[16,128]{1,0:T(8,128)} custom-call(f32[16,128]{1,0:T(8,128)} %pad.4.part), custom_call_target="tpu_custom_call" | custom-call | tf_op jit(solution)/shard_map/sum_all/pallas_call | solution.py:192
  195.3 0.8 copy.11
  196.1 0.7 fusion.12
  196.8 0.1 copy.12
  196.9 1.5 cholesky.16
  198.4 0.6 compare_reduce_fusion
  199.0 0.6 fusion.9
  199.7 1.2 custom-call.7
  200.9 3.2 %fusion = f32[16,32000]{1,0:T(8,128)} fusion(f32[1,16,32000]{2,0,1:T(1,128)S(1)} %all-to-all-done, f32[1,16,16]{1,2,0:T(8,128)S(1)} %custom-call.7), kind=kOutput, calls=%fused_computation | convolution fusion | flops 98304000 | bytes 4097024 | tf_op jit(solution)/shard_map/jit(_solve_triangular)/triangular_solve | solution.py:325
  (2 shorter events, 0.0 us)
Async XLA Ops:
  91.8 1.3 copy-start.1
  93.1 1.0 copy-start.2
  94.1 6.5 %copy-start.4 = (f32[80,256]{1,0:T(8,128)S(1)}, f32[80,256]{1,0:T(8,128)}, u32[]{:S(2)}) copy-start(f32[80,256]{1,0:T(8,128)} %constant.66.clone.row_squares) | copy-start | bytes 245764
  94.1 6.5 %copy-start.5 = (bf16[128,256]{1,0:T(8,128)(2,1)S(1)}, bf16[128,256]{1,0:T(8,128)(2,1)}, u32[]{:S(2)}) copy-start(bf16[128,256]{1,0:T(8,128)(2,1)} %constant.65.clone.inverse_right) | copy-start | bytes 196612
  94.1 6.5 %copy-start.6 = (bf16[80,256]{1,0:T(8,128)(2,1)S(1)}, bf16[80,256]{1,0:T(8,128)(2,1)}, u32[]{:S(2)}) copy-start(bf16[80,256]{1,0:T(8,128)(2,1)} %constant.64.clone.forward_right) | copy-start | bytes 122884
  94.2 6.5 %copy-start.7 = (bf16[80,240]{1,0:T(8,128)(2,1)S(1)}, bf16[80,240]{1,0:T(8,128)(2,1)}, u32[]{:S(2)}) copy-start(bf16[80,240]{1,0:T(8,128)(2,1)} %constant.63.clone.inverse_left) | copy-start | bytes 115204
  94.2 6.5 %copy-start.8 = (bf16[80,240]{1,0:T(8,128)(2,1)S(1)}, bf16[80,240]{1,0:T(8,128)(2,1)}, u32[]{:S(2)}) copy-start(bf16[80,240]{1,0:T(8,128)(2,1)} %constant.62.clone.forward_left) | copy-start | bytes 115204
  94.2 6.5 %copy-start.9 = (f32[1,256]{1,0:T(1,128)S(1)}, f32[1,256]{1,0:T(1,128)}, u32[]{:S(2)}) copy-start(f32[1,256]{1,0:T(1,128)} %constant.67.clone.lane_squares) | copy-start | bytes 3076
  100.7 1.4 copy-start
  128.3 11.1 %copy-start.3 = (bf16[16,8,4000]{2,1,0:T(8,128)(2,1)S(1)}, bf16[16,8,4000]{2,1,0:T(8,128)(2,1)}, u32[]{:S(2)}) copy-start(bf16[16,8,4000]{2,1,0:T(8,128)(2,1)} %copy-done.2) | copy-start | bytes 3072004
  128.3 49.5 %all-to-all-start = ((f32[1,16,32000]{2,0,1:T(1,128)}), f32[1,16,32000]{2,0,1:T(1,128)S(1)}, u32[]{:S(2)}, u32[]{:S(2)}) async-start(f32[1,16,32000]{2,0,1:T(1,128)} %all_to_all.15), calls=%async_computation | async-start | bytes 4096000 | tf_op jit(solution)/shard_map/all_to_all | solution.py:317

commit v2 on v1

--- a/solution.py
+++ b/solution.py
@@ -64,8 +64,7 @@
     )
 
 
-def share_kernel(count, row, slabs, partners, gathered, first_send, column_send, plane_send,
-                 receive, own_sem, slab_send, slab_receive, slab_own):
+def share_kernel(count, row, partners, first_send, column_send, plane_send, receive, own_sem):
     me = lax.axis_index("band")
     planes = count // QUARTERS
     stride = count // NP
@@ -88,11 +87,6 @@
         return remote(partners.at[r, column], partners.at[r, column],
                       plane_send.at[r, step - 1], receive.at[r, column], other)
 
-    def slab(step):
-        other = lax.rem(me + step, count)
-        return remote(slabs.at[other], gathered.at[me], slab_send.at[step - 1],
-                      slab_receive.at[step - 1], other)
-
     def arrived(r, q):
         remote(partners.at[r, q], partners.at[r, q], plane_send.at[r, 0],
                receive.at[r, q], me).wait_recv()
@@ -119,11 +113,6 @@
         for step in range(1, QUARTERS):
             across(r, step).start()
 
-    mine = pltpu.make_async_copy(slabs.at[me], gathered.at[me], slab_own)
-    mine.start()
-    for step in range(1, count):
-        slab(step).start()
-
     for r in range(NP):
         for step in range(1, QUARTERS):
             arrived(r, lax.rem(column + step, QUARTERS))
@@ -140,32 +129,26 @@
 
         for step in range(1, QUARTERS):
             across(r, step).wait_send()
-    mine.wait()
-    for step in range(1, count):
-        slab(step).wait()
-
-
-def share(row, slabs, count):
+
+
+def share(row, count):
     planes = count // QUARTERS
     anywhere = pl.BlockSpec(memory_space=pl.ANY)
     dma = pltpu.SemaphoreType.DMA
     return pl.pallas_call(
         functools.partial(share_kernel, count),
-        out_shape=(
-            jax.ShapeDtypeStruct((NP,) + row.shape, row.dtype),
-            jax.ShapeDtypeStruct(slabs.shape, slabs.dtype),
-        ),
-        in_specs=[anywhere] * 2,
-        out_specs=(anywhere, anywhere),
+        out_shape=jax.ShapeDtypeStruct((NP,) + row.shape, row.dtype),
+        in_specs=[anywhere],
+        out_specs=anywhere,
         scratch_shapes=[
             dma((NP, QUARTERS - 1)), dma((NP, planes - 1)), dma((NP, QUARTERS - 1)),
-            dma((NP, QUARTERS)), dma, dma((count - 1,)), dma((count - 1,)), dma,
+            dma((NP, QUARTERS)), dma,
         ],
         compiler_params=pltpu.CompilerParams(
             collective_id=0, has_side_effects=True, vmem_limit_bytes=1 << 20
         ),
         name="share",
-    )(row, slabs)
+    )(row)
 
 
 def sum_kernel(count, part, total, held, send, receive):
@@ -203,6 +186,30 @@
         name="sum_all",
     )(padded)
     return total[:, :columns]
+
+
+def pick_kernel(orbitals, first, last):
+    owned, width = orbitals.shape
+    values = orbitals[...].astype(jnp.float32)
+    first[...] = values[0:1].reshape(width // PAD, PAD).astype(first.dtype)
+    last[...] = values[owned - 1 : owned].reshape(width // PAD, PAD).astype(last.dtype)
+
+
+def pick(orbitals):
+    owned, points = orbitals.shape
+    steps = 10
+    width = points // steps
+    row = jax.ShapeDtypeStruct((points // PAD, PAD), orbitals.dtype)
+    spec = pl.BlockSpec((width // PAD, PAD), lambda i: (i, 0))
+    return pl.pallas_call(
+        pick_kernel,
+        grid=(steps,),
+        out_shape=(row, row),
+        in_specs=[pl.BlockSpec((owned, width), lambda i: (0, i))],
+        out_specs=(spec, spec),
+        compiler_params=pltpu.CompilerParams(vmem_limit_bytes=32 << 20),
+        name="pick",
+    )(orbitals)
 
 
 def split(values):
@@ -307,12 +314,13 @@
 
 def body(orbitals):
     devices = lax.axis_size("band")
-    owned_rows = orbitals.shape[0]
     points = orbitals.shape[1]
-    target = orbitals[0]
-    row = orbitals[owned_rows - 1].reshape(QUARTERS, points // QUARTERS // PAD, PAD)
-    slabs = target.reshape(devices, 8, points // devices // 8)
-    partners, target_slab = share(row, slabs, devices)
+    target, row = pick(orbitals)
+    partners = share(row.reshape(QUARTERS, points // QUARTERS // PAD, PAD), devices)
+    ready, partners = lax.optimization_barrier((target, partners))
+    target_slab = lax.all_to_all(
+        ready.reshape(1, points), "band", split_axis=1, concat_axis=0, tiled=True
+    )
     vectors = exchange(target.reshape(NG, NG, NG), partners.reshape(NP, NG, NG, NG))
     vector_slab = lax.all_to_all(
         vectors.reshape(1, points), "band", split_axis=1, concat_axis=0, tiled=True

time: 205 us -> 187 us (0.912)
  local copies, waits for them, and re-layouts: 46.8 us -> 28.2 us
  Pallas kernels: 99.7 us -> 83.5 us
  starting transfers between devices: 11 us -> 23.1 us
  other arithmetic: 4.71 us -> 13.5 us
  waiting for transfers between devices: 35.8 us -> 32 us
    slice x1 -> x0, local copies, waits for them, and re-layouts: 23.6 us -> none  [body(): orbitals[owned_rows - 1].reshape(QUARTERS, points // QUARTERS // PAD, PAD)]
    all_to_all x0 -> x1, starting transfers between devices: none -> 16.3 us  [body(): lax.all_to_all(ready.reshape(1, points), 'band', split_axis=1, concat_axi...]
    pallas_call x1 -> x2, Pallas kernels: 64.1 us -> 48 us  [the longest x1 46.6 us: share(): pl.pallas_call(functools.partial(share_kernel, count), out_shape=jax.Shap...]
    unnamed x20 -> x19, local copies, waits for them, and re-layouts: 3.76 us -> 12.7 us
    unnamed x0 -> x1, other arithmetic: none -> 8.77 us
    all_to_all x1, starting transfers between devices: 11 us -> 6.86 us  [body(): lax.all_to_all(vectors.reshape(1, points), 'band', split_axis=1, concat_a...]
    another operation x2 -> x0, local copies, waits for them, and re-layouts: 4.12 us -> none  [the longest x1 2.63 us: body(): target.reshape(NG, NG, NG)]
    all_to_all x1, waiting for transfers between devices: 35.8 us -> 32 us  [body(): lax.all_to_all(vectors.reshape(1, points), 'band', split_axis=1, concat_a...]
  transfers between devices with their start and end apart: 1 -> 2, of which waited for: 1 -> 1; matrix products, arithmetic and copies ran while one was open for 1% -> 7% of each run, Pallas kernels for 0% -> 11%
where the time goes in v2:
time: 187 us
  Pallas kernels  83.5 us (45%)
  waiting for transfers between devices  32 us (17%)
  local copies, waits for them, and re-layouts  28.2 us (15%)
  starting transfers between devices  23.1 us (12%)
  other arithmetic  13.5 us (7%)
  matrix products  6.2 us (3%)
    pallas_call x1, Pallas kernels, share(): pl.pallas_call(functools.partial(share_kernel, count), out_shape=jax.Shap...  46.6 us
    all_to_all x1, waiting for transfers between devices, body(): lax.all_to_all(vectors.reshape(1, points), 'band', split_axis=1, concat_a...  32 us
    pallas_call x1, Pallas kernels, exchange(): pl.pallas_call(exchange_kernel, out_shape=jax.ShapeDtypeStruct((NG, NG, N...  21.4 us
    all_to_all x1, starting transfers between devices, body(): lax.all_to_all(ready.reshape(1, points), 'band', split_axis=1, concat_axi...  16.3 us
    pallas_call x1, Pallas kernels, sum_all(): pl.pallas_call(functools.partial(sum_kernel, count), out_shape=jax.ShapeD...  14.1 us
    unnamed x19, local copies, waits for them, and re-layouts  12.7 us
    unnamed x1, other arithmetic  8.77 us
    all_to_all x1, starting transfers between devices, body(): lax.all_to_all(vectors.reshape(1, points), 'band', split_axis=1, concat_a...  6.86 us
  transfers between devices with their start and end apart: 2, of which 1 were waited for; matrix products, arithmetic and copies ran while one was open for 7% of the time, Pallas kernels for 11%

profile of v2, /device:TPU:0, one launch (start us, length us, event | category | flops | bytes accessed | tf_op | source)
XLA Modules:
  0.0 186.6 jit_solution(9404153468286149691)
XLA Ops:
  0.0 0.0 copy-start.1
  0.0 2.2 %copy-done.1 = bf16[4,512000]{1,0:T(4,128)(2,1)S(1)} copy-done((bf16[4,512000]{1,0:T(4,128)(2,1)S(1)}, bf16[4,512000]{1,0:T(4,128)(2,1)}, u32[]{:S(2)}) %copy-start.1) | copy-done | bytes 4096024
  2.2 1.4 pick.1
  3.6 46.6 %share.1 = bf16[2,4,1000,128]{3,2,1,0:T(8,128)(2,1)S(1)} custom-call(bf16[4,1000,128]{2,1,0:T(8,128)(2,1)S(1)} %bitcast.29), custom_call_target="tpu_custom_call" | custom-call | tf_op jit(solution)/shard_map/share/pallas_call | solution.py:138
  50.2 2.0 %all_to_all.30 = bf16[1,16,32000]{2,0,1:T(2,128)(2,1)} reshape(bf16[4000,128]{1,0:T(8,128)(2,1)S(1)} %get-tuple-element.11) | data formatting | bytes 2048000 | tf_op jit(solution)/shard_map/all_to_all | solution.py:321
  52.1 0.5 broadcast.56
  52.6 8.8 %reduce.6 = bf16[16,32000]{1,0:T(8,128)(2,1)} reduce(bf16[16,1,32000]{2,1,0:T(2,128)(2,1)} %bitcast.30, bf16[]{:T(256)} %broadcast.56), dimensions={1}, to_apply=%bitcast.26.reduce_sub_computation | reduce | bytes 2048002
  61.4 2.4 %reshape.38 = bf16[16,2,16000]{2,1,0:T(2,128)(2,1)} reshape(bf16[16,32000]{1,0:T(8,128)(2,1)} %reduce.6) | data formatting | bytes 2048000
  63.8 16.3 %all-to-all-start = ((bf16[16,2,16000]{2,1,0:T(2,128)(2,1)}), bf16[16,2,16000]{2,1,0:T(2,128)(2,1)}, u32[]{:S(2)}, u32[]{:S(2)}) async-start(bf16[16,2,16000]{2,1,0:T(2,128)(2,1)} %reshape.38), calls=%async_computation | async-start | bytes 2048000 | tf_op jit(solution)/shard_map/all_to_all | solution.py:321
  80.1 2.6 %reshape.36.target = bf16[80,80,80]{2,1,0:T(8,128)(2,1)} reshape(bf16[4000,128]{1,0:T(8,128)(2,1)S(1)} %get-tuple-element.11) | data formatting | bytes 2048000 | tf_op jit(solution)/shard_map/reshape | solution.py:324
  82.7 0.0 copy-start.2
  82.7 0.0 copy-start.3
  82.7 0.0 copy-start.4
  82.7 0.0 copy-start.5
  82.7 0.0 copy-start.6
  82.8 0.0 copy-start.7
  82.8 4.6 %reshape.37.partners = bf16[2,80,80,80]{3,2,1,0:T(8,128)(2,1)} reshape(bf16[2,4,1000,128]{3,2,1,0:T(8,128)(2,1)S(1)} %share.1) | data formatting | bytes 4096000 | tf_op jit(solution)/shard_map/reshape | solution.py:324
  87.4 0.0 copy-done.2
  87.4 0.0 copy-done.3
  87.4 0.0 copy-done.4
  87.4 0.0 copy-done.5
  87.4 0.0 copy-done.6
  87.4 0.0 copy-done.7
  87.5 0.0 copy-start
  87.5 1.4 copy-done
  88.9 21.4 %exchange.1 = f32[80,80,80]{2,1,0:T(8,128)S(1)} custom-call(bf16[80,80,80]{2,1,0:T(8,128)(2,1)S(1)} %copy-done, bf16[2,80,80,80]{3,2,1,0:T(8,128)(2,1)} %reshape.37.partners, bf16[80,240]{1,0:T(8,128)(2,1)S(1)} %copy-done.4, bf16[80,240]{1,0:T(8,128)(2,1)S(1)} %copy-done.5, bf16[80,256]{1,0:T(8,128)(2,1)S(1)} %copy-done.6, bf16[128,256]{1,0:T(8,128)(2,1)S(1)} %copy-done.3, ...), custom_call_target="tpu_custom_call" | custom-call | flops 983040000 | bytes 8388608 | tf_op jit(solution)/shard_map/exchange/pallas_call | solution.py:292
  110.3 4.8 %all_to_all.31 = f32[1,16,32000]{2,0,1:T(1,128)} reshape(f32[80,80,80]{2,1,0:T(8,128)S(1)} %exchange.1) | data formatting | bytes 4096000 | tf_op jit(solution)/shard_map/all_to_all | solution.py:325
  115.1 0.0 all-to-all-done
  115.1 6.9 %all-to-all-start.1 = ((f32[1,16,32000]{2,0,1:T(1,128)}), f32[1,16,32000]{2,0,1:T(1,128)S(1)}, u32[]{:S(2)}, u32[]{:S(2)}) async-start(f32[1,16,32000]{2,0,1:T(1,128)} %all_to_all.31), calls=%async_computation.1 | async-start | bytes 4096000 | tf_op jit(solution)/shard_map/all_to_all | solution.py:325
  122.0 6.2 %reshape.39 = bf16[16,1,32000]{2,1,0:T(2,128)(2,1)} reshape(bf16[16,2,16000]{2,1,0:T(2,128)(2,1)} %all-to-all-done) | data formatting | bytes 2048000
  128.2 32.0 %all-to-all-done.1 = f32[1,16,32000]{2,0,1:T(1,128)S(1)} async-done(((f32[1,16,32000]{2,0,1:T(1,128)}), f32[1,16,32000]{2,0,1:T(1,128)S(1)}, u32[]{:S(2)}, u32[]{:S(2)}) %all-to-all-start.1) | async-done | bytes 2048032 | tf_op jit(solution)/shard_map/all_to_all | solution.py:325
  160.1 3.0 %fusion.6 = f32[16,16]{1,0:T(8,128)S(1)} fusion(f32[1,16,32000]{2,0,1:T(1,128)S(1)} %all-to-all-done.1, bf16[1,16,32000]{2,0,1:T(2,128)(2,1)} %bitcast.31), kind=kOutput, calls=%fused_computation.6 | convolution fusion | flops 98304256 | bytes 3073024 | tf_op jit(solution)/shard_map/ap,bp->ab/dot_general | solution.py:329
  163.1 0.6 pad.4.part
  163.8 14.1 %sum_all.1 = f32[16,128]{1,0:T(8,128)} custom-call(f32[16,128]{1,0:T(8,128)} %pad.4.part), custom_call_target="tpu_custom_call" | custom-call | tf_op jit(solution)/shard_map/sum_all/pallas_call | solution.py:175
  177.9 0.8 copy.16
  178.6 0.7 fusion.14
  179.3 0.1 copy.17
  179.4 1.5 cholesky.16
  180.9 0.6 compare_reduce_fusion
  181.5 0.6 fusion.11
  182.2 1.2 custom-call.7
  183.4 3.2 %fusion = f32[16,32000]{1,0:T(8,128)} fusion(f32[1,16,32000]{2,0,1:T(1,128)S(1)} %all-to-all-done.1, f32[1,16,16]{1,2,0:T(8,128)S(1)} %custom-call.7), kind=kOutput, calls=%fused_computation | convolution fusion | flops 98304000 | bytes 4097024 | tf_op jit(solution)/shard_map/jit(_solve_triangular)/triangular_solve | solution.py:333
  (2 shorter events, 0.0 us)
Async XLA Ops:
  0.0 2.2 %copy-start.1 = (bf16[4,512000]{1,0:T(4,128)(2,1)S(1)}, bf16[4,512000]{1,0:T(4,128)(2,1)}, u32[]{:S(2)}) copy-start(bf16[4,512000]{1,0:T(4,128)(2,1)} %orbitals.1) | copy-start | bytes 12288004
  63.8 51.3 %all-to-all-start = ((bf16[16,2,16000]{2,1,0:T(2,128)(2,1)}), bf16[16,2,16000]{2,1,0:T(2,128)(2,1)}, u32[]{:S(2)}, u32[]{:S(2)}) async-start(bf16[16,2,16000]{2,1,0:T(2,128)(2,1)} %reshape.38), calls=%async_computation | async-start | bytes 2048000 | tf_op jit(solution)/shard_map/all_to_all | solution.py:321
  82.7 4.7 %copy-start.2 = (f32[80,256]{1,0:T(8,128)S(1)}, f32[80,256]{1,0:T(8,128)}, u32[]{:S(2)}) copy-start(f32[80,256]{1,0:T(8,128)} %constant.66.clone.row_squares) | copy-start | bytes 245764
  82.7 4.7 %copy-start.3 = (bf16[128,256]{1,0:T(8,128)(2,1)S(1)}, bf16[128,256]{1,0:T(8,128)(2,1)}, u32[]{:S(2)}) copy-start(bf16[128,256]{1,0:T(8,128)(2,1)} %constant.65.clone.inverse_right) | copy-start | bytes 196612
  82.7 4.7 %copy-start.4 = (bf16[80,240]{1,0:T(8,128)(2,1)S(1)}, bf16[80,240]{1,0:T(8,128)(2,1)}, u32[]{:S(2)}) copy-start(bf16[80,240]{1,0:T(8,128)(2,1)} %constant.62.clone.forward_left) | copy-start | bytes 115204
  82.7 4.7 %copy-start.5 = (bf16[80,240]{1,0:T(8,128)(2,1)S(1)}, bf16[80,240]{1,0:T(8,128)(2,1)}, u32[]{:S(2)}) copy-start(bf16[80,240]{1,0:T(8,128)(2,1)} %constant.63.clone.inverse_left) | copy-start | bytes 115204
  82.7 4.7 %copy-start.6 = (bf16[80,256]{1,0:T(8,128)(2,1)S(1)}, bf16[80,256]{1,0:T(8,128)(2,1)}, u32[]{:S(2)}) copy-start(bf16[80,256]{1,0:T(8,128)(2,1)} %constant.64.clone.forward_right) | copy-start | bytes 122884
  82.8 4.7 %copy-start.7 = (f32[1,256]{1,0:T(1,128)S(1)}, f32[1,256]{1,0:T(1,128)}, u32[]{:S(2)}) copy-start(f32[1,256]{1,0:T(1,128)} %constant.67.clone.lane_squares) | copy-start | bytes 3076
  87.5 1.4 copy-start
  115.1 45.0 %all-to-all-start.1 = ((f32[1,16,32000]{2,0,1:T(1,128)}), f32[1,16,32000]{2,0,1:T(1,128)S(1)}, u32[]{:S(2)}, u32[]{:S(2)}) async-start(f32[1,16,32000]{2,0,1:T(1,128)} %all_to_all.31), calls=%async_computation.1 | async-start | bytes 4096000 | tf_op jit(solution)/shard_map/all_to_all | solution.py:325

commit v3 on v2

--- a/solution.py
+++ b/solution.py
@@ -234,9 +234,21 @@
     return both[:, :PAD] + both[:, PAD:] + dot(low, table[:, :PAD])
 
 
-def exchange_kernel(target, partners, forward_left, inverse_left, forward_right, inverse_right,
-                    row_squares, lane_squares, vectors, one, two):
+def exchange_kernel(count, target, partners, forward_left, inverse_left, forward_right,
+                    inverse_right, row_squares, lane_squares, slabs, vectors, gathered, one, two,
+                    send, receive, own_sem):
     group = 8
+    me = lax.axis_index("band")
+    barrier_all(me, count)
+
+    def slab(step):
+        other = lax.rem(me + step, count)
+        return remote(slabs.at[other], gathered.at[me], send.at[step], receive.at[step], other)
+
+    for step in range(1, count):
+        slab(step).start()
+    own = pltpu.make_async_copy(slabs.at[me], gathered.at[me], own_sem)
+    own.start()
 
     def ahead(step, carry):
         planes = pl.ds(step * group, group)
@@ -282,20 +294,31 @@
         return carry
 
     lax.fori_loop(0, NG // group, back, 0)
-
-
-def exchange(target, partners):
+    own.wait()
+    for step in range(1, count):
+        slab(step).wait()
+
+
+def exchange(target, partners, slabs, count):
     fourier, squares = tables(NG)
     lanes = np.zeros((PAD,), np.float32)
     lanes[:NG] = squares
     vmem = pl.BlockSpec(memory_space=pltpu.VMEM)
+    anywhere = pl.BlockSpec(memory_space=pl.ANY)
+    dma = pltpu.SemaphoreType.DMA
     return pl.pallas_call(
-        exchange_kernel,
-        out_shape=jax.ShapeDtypeStruct((NG, NG, NG), jnp.float32),
-        in_specs=[vmem] * 8,
-        out_specs=vmem,
-        scratch_shapes=[pltpu.VMEM((NG, NG, NP * PAD), jnp.float32)] * 2,
-        compiler_params=pltpu.CompilerParams(vmem_limit_bytes=48 << 20),
+        functools.partial(exchange_kernel, count),
+        out_shape=(
+            jax.ShapeDtypeStruct((NG, NG, NG), jnp.float32),
+            jax.ShapeDtypeStruct(slabs.shape, slabs.dtype),
+        ),
+        in_specs=[vmem] * 8 + [anywhere],
+        out_specs=(vmem, anywhere),
+        scratch_shapes=[pltpu.VMEM((NG, NG, NP * PAD), jnp.float32)] * 2
+        + [dma((count,)), dma((count,)), dma],
+        compiler_params=pltpu.CompilerParams(
+            collective_id=2, has_side_effects=True, vmem_limit_bytes=48 << 20
+        ),
         cost_estimate=pl.CostEstimate(
             flops=12 * NP * NG**4, bytes_accessed=8 << 20, transcendentals=0
         ),
@@ -309,6 +332,7 @@
         right_table(fourier, PAD),
         np.broadcast_to(squares[:, None], (NG, NP * PAD)).copy(),
         np.tile(lanes, NP)[None, :],
+        slabs,
     )
 
 
@@ -317,11 +341,12 @@
     points = orbitals.shape[1]
     target, row = pick(orbitals)
     partners = share(row.reshape(QUARTERS, points // QUARTERS // PAD, PAD), devices)
-    ready, partners = lax.optimization_barrier((target, partners))
-    target_slab = lax.all_to_all(
-        ready.reshape(1, points), "band", split_axis=1, concat_axis=0, tiled=True
-    )
-    vectors = exchange(target.reshape(NG, NG, NG), partners.reshape(NP, NG, NG, NG))
+    vectors, target_slab = exchange(
+        target.reshape(NG, NG, NG),
+        partners.reshape(NP, NG, NG, NG),
+        target.reshape(devices, 8, points // devices // 8),
+        devices,
+    )
     vector_slab = lax.all_to_all(
         vectors.reshape(1, points), "band", split_axis=1, concat_axis=0, tiled=True
     )

time: 187 us -> 181 us (0.968)
  Pallas kernels: 83.5 us -> 101 us
  starting transfers between devices: 23.1 us -> 6.13 us
  other arithmetic: 13.5 us -> 4.71 us
  waiting for transfers between devices: 32 us -> 38.6 us
  local copies, waits for them, and re-layouts: 28.2 us -> 24.6 us
    pallas_call x1, Pallas kernels: 21.4 us -> 38.4 us  [exchange(): pl.pallas_call(functools.partial(exchange_kernel, count), out_shape=(jax....]
    all_to_all x1 -> x0, starting transfers between devices: 16.3 us -> none  [body(): lax.all_to_all(ready.reshape(1, points), 'band', split_axis=1, concat_axi...]
    unnamed x1 -> x0, other arithmetic: 8.77 us -> none
    unnamed x19 -> x20, local copies, waits for them, and re-layouts: 12.7 us -> 5.8 us
    all_to_all x1, waiting for transfers between devices: 32 us -> 38.6 us  [body(): lax.all_to_all(vectors.reshape(1, points), 'band', split_axis=1, concat_a...]
    reshape x0 -> x2, local copies, waits for them, and re-layouts: none -> 4.06 us  [the longest x1 2.59 us: body(): target_slab.reshape(devices, points // devices).astype(jnp.float32)]
    all_to_all x1 -> x0, local copies, waits for them, and re-layouts: 1.96 us -> none  [body(): lax.all_to_all(ready.reshape(1, points), 'band', split_axis=1, concat_axi...]
  transfers between devices with their start and end apart: 2 -> 1, of which waited for: 1 -> 1; matrix products, arithmetic and copies ran while one was open for 7% -> 1% of each run, Pallas kernels for 11% -> 0%
where the time goes in v3:
time: 181 us
  Pallas kernels  101 us (56%)
  waiting for transfers between devices  38.6 us (21%)
  local copies, waits for them, and re-layouts  24.6 us (14%)
  starting transfers between devices  6.13 us (3%)
  matrix products  5.85 us (3%)
  other arithmetic  4.71 us (3%)
    pallas_call x1, Pallas kernels, share(): pl.pallas_call(functools.partial(share_kernel, count), out_shape=jax.Shap...  46.5 us
    all_to_all x1, waiting for transfers between devices, body(): lax.all_to_all(vectors.reshape(1, points), 'band', split_axis=1, concat_a...  38.6 us
    pallas_call x1, Pallas kernels, exchange(): pl.pallas_call(functools.partial(exchange_kernel, count), out_shape=(jax....  38.4 us
    pallas_call x1, Pallas kernels, sum_all(): pl.pallas_call(functools.partial(sum_kernel, count), out_shape=jax.ShapeD...  14.2 us
    all_to_all x1, starting transfers between devices, body(): lax.all_to_all(vectors.reshape(1, points), 'band', split_axis=1, concat_a...  6.13 us
    all_to_all x1, local copies, waits for them, and re-layouts, body(): lax.all_to_all(vectors.reshape(1, points), 'band', split_axis=1, concat_a...  5.99 us
    unnamed x20, local copies, waits for them, and re-layouts  5.8 us
    reshape x1, local copies, waits for them, and re-layouts, body(): partners.reshape(NP, NG, NG, NG)  4.64 us
  transfers between devices with their start and end apart: 1, of which 1 were waited for; matrix products, arithmetic and copies ran while one was open for 1% of the time, Pallas kernels for 0%

profile of v3, /device:TPU:0, one launch (start us, length us, event | category | flops | bytes accessed | tf_op | source)
XLA Modules:
  0.0 180.6 jit_solution(10448299018139358463)
XLA Ops:
  0.0 0.0 copy-start.1
  0.0 2.2 %copy-done.1 = bf16[4,512000]{1,0:T(4,128)(2,1)S(1)} copy-done((bf16[4,512000]{1,0:T(4,128)(2,1)S(1)}, bf16[4,512000]{1,0:T(4,128)(2,1)}, u32[]{:S(2)}) %copy-start.1) | copy-done | bytes 4096024
  2.2 1.4 pick.1
  3.6 0.0 copy-start.2
  3.6 1.0 copy-done.2
  4.5 1.5 reshape.36.slabs
  6.0 2.6 %reshape.33.target = bf16[80,80,80]{2,1,0:T(8,128)(2,1)} reshape(bf16[4000,128]{1,0:T(8,128)(2,1)S(1)} %get-tuple-element.9) | data formatting | bytes 2048000 | tf_op jit(solution)/shard_map/reshape | solution.py:345
  8.6 0.0 copy-start.3
  8.6 1.2 copy-done.3
  9.9 46.5 %share.1 = bf16[2,4,1000,128]{3,2,1,0:T(8,128)(2,1)S(1)} custom-call(bf16[4,1000,128]{2,1,0:T(8,128)(2,1)S(1)} %bitcast.25), custom_call_target="tpu_custom_call" | custom-call | tf_op jit(solution)/shard_map/share/pallas_call | solution.py:138
  56.4 0.0 copy-start.4
  56.4 0.0 copy-start.5
  56.4 0.0 copy-start.6
  56.4 0.0 copy-start.7
  56.5 0.0 copy-start.8
  56.5 0.0 copy-start.9
  56.5 4.6 %reshape.35.partners = bf16[2,80,80,80]{3,2,1,0:T(8,128)(2,1)} reshape(bf16[2,4,1000,128]{3,2,1,0:T(8,128)(2,1)S(1)} %share.1) | data formatting | bytes 4096000 | tf_op jit(solution)/shard_map/reshape | solution.py:346
  61.1 0.0 copy-done.4
  61.1 0.0 copy-done.5
  61.1 0.0 copy-done.6
  61.1 0.0 copy-done.7
  61.1 0.0 copy-done.8
  61.2 0.0 copy-done.9
  61.2 0.0 copy-start
  61.2 1.4 copy-done
  62.6 38.4 %exchange.1 = (f32[80,80,80]{2,1,0:T(8,128)}, bf16[16,8,4000]{2,1,0:T(8,128)(2,1)S(1)}) custom-call(bf16[80,80,80]{2,1,0:T(8,128)(2,1)S(1)} %copy-done, bf16[2,80,80,80]{3,2,1,0:T(8,128)(2,1)} %reshape.35.partners, bf16[80,240]{1,0:T(8,128)(2,1)S(1)} %copy-done.8, bf16[80,240]{1,0:T(8,128)(2,1)S(1)} %copy-done.7, bf16[80,256]{1,0:T(8,128)(2,1)S(1)} %copy-done.6, ...), custom_call_target="tpu_custom_call" | custom-call | flops 983040000 | bytes 8388608 | tf_op jit(solution)/shard_map/exchange/pallas_call | solution.py:309
  101.0 6.0 %all_to_all.15 = f32[1,16,32000]{2,0,1:T(1,128)} reshape(f32[80,80,80]{2,1,0:T(8,128)} %get-tuple-element.12) | data formatting | bytes 4096000 | tf_op jit(solution)/shard_map/all_to_all | solution.py:350
  107.0 6.1 %all-to-all-start = ((f32[1,16,32000]{2,0,1:T(1,128)}), f32[1,16,32000]{2,0,1:T(1,128)S(1)}, u32[]{:S(2)}, u32[]{:S(2)}) async-start(f32[1,16,32000]{2,0,1:T(1,128)} %all_to_all.15), calls=%async_computation | async-start | bytes 4096000 | tf_op jit(solution)/shard_map/all_to_all | solution.py:350
  113.1 2.6 %reshape.37 = bf16[16,32000]{1,0:T(8,128)(2,1)} reshape(bf16[16,8,4000]{2,1,0:T(8,128)(2,1)S(1)} %get-tuple-element.11) | data formatting | bytes 2048000 | tf_op jit(solution)/shard_map/reshape | solution.py:353
  115.7 38.6 %all-to-all-done = f32[1,16,32000]{2,0,1:T(1,128)S(1)} async-done(((f32[1,16,32000]{2,0,1:T(1,128)}), f32[1,16,32000]{2,0,1:T(1,128)S(1)}, u32[]{:S(2)}, u32[]{:S(2)}) %all-to-all-start) | async-done | bytes 2048032 | tf_op jit(solution)/shard_map/all_to_all | solution.py:350
  154.4 2.7 %fusion.6 = f32[16,16]{1,0:T(8,128)S(1)} fusion(bf16[16,32000]{1,0:T(8,128)(2,1)} %reshape.37, f32[1,16,32000]{2,0,1:T(1,128)S(1)} %all-to-all-done), kind=kOutput, calls=%fused_computation.6 | convolution fusion | flops 98304256 | bytes 3073024 | tf_op jit(solution)/shard_map/ap,bp->ab/dot_general | solution.py:354
  157.0 0.6 pad.4.part
  157.7 14.2 %sum_all.1 = f32[16,128]{1,0:T(8,128)} custom-call(f32[16,128]{1,0:T(8,128)} %pad.4.part), custom_call_target="tpu_custom_call" | custom-call | tf_op jit(solution)/shard_map/sum_all/pallas_call | solution.py:175
  171.9 0.8 copy.11
  172.7 0.7 fusion.12
  173.4 0.1 copy.12
  173.4 1.5 cholesky.16
  174.9 0.6 compare_reduce_fusion
  175.6 0.6 fusion.9
  176.2 1.2 custom-call.7
  177.5 3.2 %fusion = f32[16,32000]{1,0:T(8,128)} fusion(f32[1,16,32000]{2,0,1:T(1,128)S(1)} %all-to-all-done, f32[1,16,16]{1,2,0:T(8,128)S(1)} %custom-call.7), kind=kOutput, calls=%fused_computation | convolution fusion | flops 98304000 | bytes 4097024 | tf_op jit(solution)/shard_map/jit(_solve_triangular)/triangular_solve | solution.py:358
  (2 shorter events, 0.0 us)
Async XLA Ops:
  0.0 2.2 %copy-start.1 = (bf16[4,512000]{1,0:T(4,128)(2,1)S(1)}, bf16[4,512000]{1,0:T(4,128)(2,1)}, u32[]{:S(2)}) copy-start(bf16[4,512000]{1,0:T(4,128)(2,1)} %orbitals.1) | copy-start | bytes 12288004
  3.6 1.0 copy-start.2
  8.6 1.2 copy-start.3
  56.4 4.7 %copy-start.4 = (f32[80,256]{1,0:T(8,128)S(1)}, f32[80,256]{1,0:T(8,128)}, u32[]{:S(2)}) copy-start(f32[80,256]{1,0:T(8,128)} %constant.66.clone.row_squares) | copy-start | bytes 245764
  56.4 4.7 %copy-start.5 = (bf16[128,256]{1,0:T(8,128)(2,1)S(1)}, bf16[128,256]{1,0:T(8,128)(2,1)}, u32[]{:S(2)}) copy-start(bf16[128,256]{1,0:T(8,128)(2,1)} %constant.65.clone.inverse_right) | copy-start | bytes 196612
  56.4 4.7 %copy-start.6 = (bf16[80,256]{1,0:T(8,128)(2,1)S(1)}, bf16[80,256]{1,0:T(8,128)(2,1)}, u32[]{:S(2)}) copy-start(bf16[80,256]{1,0:T(8,128)(2,1)} %constant.64.clone.forward_right) | copy-start | bytes 122884
  56.4 4.7 %copy-start.7 = (bf16[80,240]{1,0:T(8,128)(2,1)S(1)}, bf16[80,240]{1,0:T(8,128)(2,1)}, u32[]{:S(2)}) copy-start(bf16[80,240]{1,0:T(8,128)(2,1)} %constant.63.clone.inverse_left) | copy-start | bytes 115204
  56.5 4.7 %copy-start.8 = (bf16[80,240]{1,0:T(8,128)(2,1)S(1)}, bf16[80,240]{1,0:T(8,128)(2,1)}, u32[]{:S(2)}) copy-start(bf16[80,240]{1,0:T(8,128)(2,1)} %constant.62.clone.forward_left) | copy-start | bytes 115204
  56.5 4.7 %copy-start.9 = (f32[1,256]{1,0:T(1,128)S(1)}, f32[1,256]{1,0:T(1,128)}, u32[]{:S(2)}) copy-start(f32[1,256]{1,0:T(1,128)} %constant.67.clone.lane_squares) | copy-start | bytes 3076
  61.2 1.4 copy-start
  107.0 47.4 %all-to-all-start = ((f32[1,16,32000]{2,0,1:T(1,128)}), f32[1,16,32000]{2,0,1:T(1,128)S(1)}, u32[]{:S(2)}, u32[]{:S(2)}) async-start(f32[1,16,32000]{2,0,1:T(1,128)} %all_to_all.15), calls=%async_computation | async-start | bytes 4096000 | tf_op jit(solution)/shard_map/all_to_all | solution.py:350

commit v4 on v3

--- a/solution.py
+++ b/solution.py
@@ -12,6 +12,7 @@
 NP = 2
 PAD = 128
 QUARTERS = 4
+CHUNKS = 5
 highest = lax.Precision.HIGHEST
 
 
@@ -73,62 +74,76 @@
     base = plane * QUARTERS
     barrier_all(me, count)
 
-    def first(r, q):
-        return remote(row.at[q], partners.at[r, q], first_send.at[r, q - 1],
-                      receive.at[r, q], lax.rem(me + q, count))
-
-    def down(r, step):
+    def first(r, q, c):
+        return remote(row.at[q, c], partners.at[r, q, c], first_send.at[q - 1, c],
+                      receive.at[r, q, c], lax.rem(me + q, count))
+
+    def down(r, step, c):
         other = lax.rem(me + step * QUARTERS, count)
-        return remote(partners.at[r, column], partners.at[r, column],
-                      column_send.at[r, step - 1], receive.at[r, column], other)
-
-    def across(r, step):
-        other = base + lax.rem(column + step, QUARTERS)
-        return remote(partners.at[r, column], partners.at[r, column],
-                      plane_send.at[r, step - 1], receive.at[r, column], other)
-
-    def arrived(r, q):
-        remote(partners.at[r, q], partners.at[r, q], plane_send.at[r, 0],
-               receive.at[r, q], me).wait_recv()
+        return remote(partners.at[r, column, c], partners.at[r, column, c],
+                      column_send.at[r, step - 1, c], receive.at[r, column, c], other)
+
+    def neighbour(step):
+        return base + lax.rem(column + step, QUARTERS)
+
+    def across(r, step, c):
+        return remote(partners.at[r, column, c], partners.at[r, column, c],
+                      plane_send.at[r, step - 1, c], receive.at[r, column, c], neighbour(step))
+
+    def arrived(r, q, c):
+        remote(partners.at[r, q, c], partners.at[r, q, c], plane_send.at[r, 0, c],
+               receive.at[r, q, c], me).wait_recv()
 
     for r in range(NP):
         @pl.when(me == r * stride)
         def _():
-            for q in range(1, QUARTERS):
-                first(r, q).start()
-            own = pltpu.make_async_copy(row.at[0], partners.at[r, 0], own_sem)
+            for c in range(CHUNKS):
+                for q in range(1, QUARTERS):
+                    first(r, q, c).start()
+            own = pltpu.make_async_copy(row, partners.at[r], own_sem)
             own.start()
             own.wait()
+
+    for c in range(CHUNKS):
+        for r in range(NP):
+            @pl.when(me != r * stride)
+            def _():
+                arrived(r, column, c)
+
+            @pl.when(plane == r * stride // QUARTERS)
+            def _():
+                for step in range(1, planes):
+                    down(r, step, c).start()
+
+            for step in range(1, QUARTERS):
+                @pl.when(neighbour(step) != r * stride)
+                def _():
+                    across(r, step, c).start()
 
     for r in range(NP):
         @pl.when(me != r * stride)
         def _():
-            arrived(r, column)
+            for c in range(CHUNKS):
+                for step in range(1, QUARTERS):
+                    arrived(r, lax.rem(column + step, QUARTERS), c)
+
+        @pl.when(me == r * stride)
+        def _():
+            for c in range(CHUNKS):
+                for q in range(1, QUARTERS):
+                    first(r, q, c).wait_send()
 
         @pl.when(plane == r * stride // QUARTERS)
         def _():
-            for step in range(1, planes):
-                down(r, step).start()
+            for c in range(CHUNKS):
+                for step in range(1, planes):
+                    down(r, step, c).wait_send()
 
         for step in range(1, QUARTERS):
-            across(r, step).start()
-
-    for r in range(NP):
-        for step in range(1, QUARTERS):
-            arrived(r, lax.rem(column + step, QUARTERS))
-    for r in range(NP):
-        @pl.when(me == r * stride)
-        def _():
-            for q in range(1, QUARTERS):
-                first(r, q).wait_send()
-
-        @pl.when(plane == r * stride // QUARTERS)
-        def _():
-            for step in range(1, planes):
-                down(r, step).wait_send()
-
-        for step in range(1, QUARTERS):
-            across(r, step).wait_send()
+            @pl.when(neighbour(step) != r * stride)
+            def _():
+                for c in range(CHUNKS):
+                    across(r, step, c).wait_send()
 
 
 def share(row, count):
@@ -141,8 +156,8 @@
         in_specs=[anywhere],
         out_specs=anywhere,
         scratch_shapes=[
-            dma((NP, QUARTERS - 1)), dma((NP, planes - 1)), dma((NP, QUARTERS - 1)),
-            dma((NP, QUARTERS)), dma,
+            dma((QUARTERS - 1, CHUNKS)), dma((NP, planes - 1, CHUNKS)),
+            dma((NP, QUARTERS - 1, CHUNKS)), dma((NP, QUARTERS, CHUNKS)), dma,
         ],
         compiler_params=pltpu.CompilerParams(
             collective_id=0, has_side_effects=True, vmem_limit_bytes=1 << 20
@@ -340,7 +355,7 @@
     devices = lax.axis_size("band")
     points = orbitals.shape[1]
     target, row = pick(orbitals)
-    partners = share(row.reshape(QUARTERS, points // QUARTERS // PAD, PAD), devices)
+    partners = share(row.reshape(QUARTERS, CHUNKS, -1, PAD), devices)
     vectors, target_slab = exchange(
         target.reshape(NG, NG, NG),
         partners.reshape(NP, NG, NG, NG),

time: 181 us -> 175 us (0.967)
  Pallas kernels: 101 us -> 97.2 us
    pallas_call x1, Pallas kernels: 38.4 us -> 25.6 us  [exchange(): pl.pallas_call(functools.partial(exchange_kernel, count), out_shape=(jax....]
    pallas_call x1, Pallas kernels: 46.5 us -> 56 us  [share(): pl.pallas_call(functools.partial(share_kernel, count), out_shape=jax.Shap...]
where the time goes in v4:
time: 175 us
  Pallas kernels  97.2 us (56%)
  waiting for transfers between devices  37.2 us (21%)
  local copies, waits for them, and re-layouts  24.6 us (14%)
  matrix products  5.85 us (3%)
  starting transfers between devices  5 us (3%)
  other arithmetic  4.71 us (3%)
    pallas_call x1, Pallas kernels, share(): pl.pallas_call(functools.partial(share_kernel, count), out_shape=jax.Shap...  56 us
    all_to_all x1, waiting for transfers between devices, body(): lax.all_to_all(vectors.reshape(1, points), 'band', split_axis=1, concat_a...  37.2 us
    pallas_call x1, Pallas kernels, exchange(): pl.pallas_call(functools.partial(exchange_kernel, count), out_shape=(jax....  25.6 us
    pallas_call x1, Pallas kernels, sum_all(): pl.pallas_call(functools.partial(sum_kernel, count), out_shape=jax.ShapeD...  14.2 us
    all_to_all x1, local copies, waits for them, and re-layouts, body(): lax.all_to_all(vectors.reshape(1, points), 'band', split_axis=1, concat_a...  5.99 us
    unnamed x20, local copies, waits for them, and re-layouts  5.8 us
    all_to_all x1, starting transfers between devices, body(): lax.all_to_all(vectors.reshape(1, points), 'band', split_axis=1, concat_a...  5 us
    reshape x1, local copies, waits for them, and re-layouts, body(): partners.reshape(NP, NG, NG, NG)  4.64 us
  transfers between devices with their start and end apart: 1, of which 1 were waited for; matrix products, arithmetic and copies ran while one was open for 1% of the time, Pallas kernels for 0%

profile of v4, /device:TPU:0, one launch (start us, length us, event | category | flops | bytes accessed | tf_op | source)
XLA Modules:
  0.0 174.7 jit_solution(4776819856003690541)
XLA Ops:
  0.0 0.0 copy-start.1
  0.0 2.2 %copy-done.1 = bf16[4,512000]{1,0:T(4,128)(2,1)S(1)} copy-done((bf16[4,512000]{1,0:T(4,128)(2,1)S(1)}, bf16[4,512000]{1,0:T(4,128)(2,1)}, u32[]{:S(2)}) %copy-start.1) | copy-done | bytes 4096024
  2.2 1.4 pick.1
  3.6 0.0 copy-start.2
  3.6 1.0 copy-done.2
  4.5 1.5 reshape.36.slabs
  6.0 2.6 %reshape.33.target = bf16[80,80,80]{2,1,0:T(8,128)(2,1)} reshape(bf16[4000,128]{1,0:T(8,128)(2,1)S(1)} %get-tuple-element.9) | data formatting | bytes 2048000 | tf_op jit(solution)/shard_map/reshape | solution.py:360
  8.6 0.0 copy-start.3
  8.6 1.2 copy-done.3
  9.9 56.0 %share.1 = bf16[2,4,5,200,128]{4,3,2,1,0:T(8,128)(2,1)S(1)} custom-call(bf16[4,5,200,128]{3,2,1,0:T(8,128)(2,1)S(1)} %bitcast.25), custom_call_target="tpu_custom_call" | custom-call | tf_op jit(solution)/shard_map/share/pallas_call | solution.py:153
  65.8 0.0 copy-start.4
  65.8 0.0 copy-start.5
  65.9 0.0 copy-start.6
  65.9 0.0 copy-start.7
  65.9 0.0 copy-start.8
  65.9 0.0 copy-start.9
  65.9 4.6 %reshape.35.partners = bf16[2,80,80,80]{3,2,1,0:T(8,128)(2,1)} reshape(bf16[2,4,5,200,128]{4,3,2,1,0:T(8,128)(2,1)S(1)} %share.1) | data formatting | bytes 4096000 | tf_op jit(solution)/shard_map/reshape | solution.py:361
  70.6 0.0 copy-done.4
  70.6 0.0 copy-done.5
  70.6 0.0 copy-done.6
  70.6 0.0 copy-done.7
  70.6 0.0 copy-done.8
  70.6 0.0 copy-done.9
  70.6 0.0 copy-start
  70.6 1.4 copy-done
  72.0 25.6 %exchange.1 = (f32[80,80,80]{2,1,0:T(8,128)}, bf16[16,8,4000]{2,1,0:T(8,128)(2,1)S(1)}) custom-call(bf16[80,80,80]{2,1,0:T(8,128)(2,1)S(1)} %copy-done, bf16[2,80,80,80]{3,2,1,0:T(8,128)(2,1)} %reshape.35.partners, bf16[80,240]{1,0:T(8,128)(2,1)S(1)} %copy-done.8, bf16[80,240]{1,0:T(8,128)(2,1)S(1)} %copy-done.7, bf16[80,256]{1,0:T(8,128)(2,1)S(1)} %copy-done.6, ...), custom_call_target="tpu_custom_call" | custom-call | flops 983040000 | bytes 8388608 | tf_op jit(solution)/shard_map/exchange/pallas_call | solution.py:324
  97.6 6.0 %all_to_all.15 = f32[1,16,32000]{2,0,1:T(1,128)} reshape(f32[80,80,80]{2,1,0:T(8,128)} %get-tuple-element.12) | data formatting | bytes 4096000 | tf_op jit(solution)/shard_map/all_to_all | solution.py:365
  103.6 5.0 %all-to-all-start = ((f32[1,16,32000]{2,0,1:T(1,128)}), f32[1,16,32000]{2,0,1:T(1,128)S(1)}, u32[]{:S(2)}, u32[]{:S(2)}) async-start(f32[1,16,32000]{2,0,1:T(1,128)} %all_to_all.15), calls=%async_computation | async-start | bytes 4096000 | tf_op jit(solution)/shard_map/all_to_all | solution.py:365
  108.6 2.6 %reshape.37 = bf16[16,32000]{1,0:T(8,128)(2,1)} reshape(bf16[16,8,4000]{2,1,0:T(8,128)(2,1)S(1)} %get-tuple-element.11) | data formatting | bytes 2048000 | tf_op jit(solution)/shard_map/reshape | solution.py:368
  111.2 37.2 %all-to-all-done = f32[1,16,32000]{2,0,1:T(1,128)S(1)} async-done(((f32[1,16,32000]{2,0,1:T(1,128)}), f32[1,16,32000]{2,0,1:T(1,128)S(1)}, u32[]{:S(2)}, u32[]{:S(2)}) %all-to-all-start) | async-done | bytes 2048032 | tf_op jit(solution)/shard_map/all_to_all | solution.py:365
  148.4 2.7 %fusion.6 = f32[16,16]{1,0:T(8,128)S(1)} fusion(bf16[16,32000]{1,0:T(8,128)(2,1)} %reshape.37, f32[1,16,32000]{2,0,1:T(1,128)S(1)} %all-to-all-done), kind=kOutput, calls=%fused_computation.6 | convolution fusion | flops 98304256 | bytes 3073024 | tf_op jit(solution)/shard_map/ap,bp->ab/dot_general | solution.py:369
  151.1 0.6 pad.4.part
  151.8 14.2 %sum_all.1 = f32[16,128]{1,0:T(8,128)} custom-call(f32[16,128]{1,0:T(8,128)} %pad.4.part), custom_call_target="tpu_custom_call" | custom-call | tf_op jit(solution)/shard_map/sum_all/pallas_call | solution.py:190
  166.0 0.8 copy.11
  166.7 0.7 fusion.12
  167.4 0.1 copy.12
  167.5 1.5 cholesky.16
  169.0 0.6 compare_reduce_fusion
  169.6 0.6 fusion.9
  170.3 1.2 custom-call.7
  171.5 3.2 %fusion = f32[16,32000]{1,0:T(8,128)} fusion(f32[1,16,32000]{2,0,1:T(1,128)S(1)} %all-to-all-done, f32[1,16,16]{1,2,0:T(8,128)S(1)} %custom-call.7), kind=kOutput, calls=%fused_computation | convolution fusion | flops 98304000 | bytes 4097024 | tf_op jit(solution)/shard_map/jit(_solve_triangular)/triangular_solve | solution.py:373
  (2 shorter events, 0.0 us)
Async XLA Ops:
  0.0 2.2 %copy-start.1 = (bf16[4,512000]{1,0:T(4,128)(2,1)S(1)}, bf16[4,512000]{1,0:T(4,128)(2,1)}, u32[]{:S(2)}) copy-start(bf16[4,512000]{1,0:T(4,128)(2,1)} %orbitals.1) | copy-start | bytes 12288004
  3.6 1.0 copy-start.2
  8.6 1.2 copy-start.3
  65.8 4.7 %copy-start.4 = (f32[80,256]{1,0:T(8,128)S(1)}, f32[80,256]{1,0:T(8,128)}, u32[]{:S(2)}) copy-start(f32[80,256]{1,0:T(8,128)} %constant.66.clone.row_squares) | copy-start | bytes 245764
  65.8 4.7 %copy-start.5 = (bf16[128,256]{1,0:T(8,128)(2,1)S(1)}, bf16[128,256]{1,0:T(8,128)(2,1)}, u32[]{:S(2)}) copy-start(bf16[128,256]{1,0:T(8,128)(2,1)} %constant.65.clone.inverse_right) | copy-start | bytes 196612
  65.9 4.7 %copy-start.6 = (bf16[80,256]{1,0:T(8,128)(2,1)S(1)}, bf16[80,256]{1,0:T(8,128)(2,1)}, u32[]{:S(2)}) copy-start(bf16[80,256]{1,0:T(8,128)(2,1)} %constant.64.clone.forward_right) | copy-start | bytes 122884
  65.9 4.7 %copy-start.7 = (bf16[80,240]{1,0:T(8,128)(2,1)S(1)}, bf16[80,240]{1,0:T(8,128)(2,1)}, u32[]{:S(2)}) copy-start(bf16[80,240]{1,0:T(8,128)(2,1)} %constant.63.clone.inverse_left) | copy-start | bytes 115204
  65.9 4.7 %copy-start.8 = (bf16[80,240]{1,0:T(8,128)(2,1)S(1)}, bf16[80,240]{1,0:T(8,128)(2,1)}, u32[]{:S(2)}) copy-start(bf16[80,240]{1,0:T(8,128)(2,1)} %constant.62.clone.forward_left) | copy-start | bytes 115204
  65.9 4.7 %copy-start.9 = (f32[1,256]{1,0:T(1,128)S(1)}, f32[1,256]{1,0:T(1,128)}, u32[]{:S(2)}) copy-start(f32[1,256]{1,0:T(1,128)} %constant.67.clone.lane_squares) | copy-start | bytes 3076
  70.6 1.4 copy-start
  103.6 44.8 %all-to-all-start = ((f32[1,16,32000]{2,0,1:T(1,128)}), f32[1,16,32000]{2,0,1:T(1,128)S(1)}, u32[]{:S(2)}, u32[]{:S(2)}) async-start(f32[1,16,32000]{2,0,1:T(1,128)} %all_to_all.15), calls=%async_computation | async-start | bytes 4096000 | tf_op jit(solution)/shard_map/all_to_all | solution.py:365

commit v5 on v4

--- a/solution.py
+++ b/solution.py
@@ -183,24 +183,22 @@
 
 
 def sum_all(part, count):
-    rows, columns = part.shape
-    width = -(-columns // PAD) * PAD
-    padded = jnp.pad(part, ((0, 0), (0, width - columns)))
     vmem = pl.BlockSpec(memory_space=pltpu.VMEM)
-    total = pl.pallas_call(
+    return pl.pallas_call(
         functools.partial(sum_kernel, count),
-        out_shape=jax.ShapeDtypeStruct((rows, width), jnp.float32),
+        out_shape=jax.ShapeDtypeStruct(part.shape, jnp.float32),
         in_specs=[vmem],
         out_specs=vmem,
         scratch_shapes=[
-            pltpu.VMEM((count, rows, width), jnp.float32),
+            pltpu.VMEM((count,) + part.shape, jnp.float32),
             pltpu.SemaphoreType.DMA((count,)),
             pltpu.SemaphoreType.DMA((count,)),
         ],
-        compiler_params=pltpu.CompilerParams(collective_id=1, has_side_effects=True),
+        compiler_params=pltpu.CompilerParams(
+            collective_id=1, has_side_effects=True, vmem_limit_bytes=4 << 20
+        ),
         name="sum_all",
-    )(padded)
-    return total[:, :columns]
+    )(part)
 
 
 def pick_kernel(orbitals, first, last):
@@ -222,7 +220,7 @@
         out_shape=(row, row),
         in_specs=[pl.BlockSpec((owned, width), lambda i: (0, i))],
         out_specs=(spec, spec),
-        compiler_params=pltpu.CompilerParams(vmem_limit_bytes=32 << 20),
+        compiler_params=pltpu.CompilerParams(vmem_limit_bytes=6 << 20),
         name="pick",
     )(orbitals)
 
@@ -369,7 +367,7 @@
     part = jnp.einsum("ap,bp->ab", target_slab, vector_slab, precision=highest) / NG**3
     intersection = sum_all(part, devices)
     metric = -0.5 * (intersection + intersection.T)
-    factor = jnp.linalg.cholesky(metric)
+    factor = lax.linalg.cholesky(metric, symmetrize_input=False)
     return jax.scipy.linalg.solve_triangular(factor, vector_slab, lower=True)
 
 

time: 175 us -> 172 us (0.983)
  transfers between devices with their start and end apart: 1 -> 1, of which waited for: 1 -> 1; matrix products, arithmetic and copies ran while one was open for 1% -> 2% of each run, Pallas kernels for 0% -> 0%
where the time goes in v5:
time: 172 us; the launch traced here: 171 us
  Pallas kernels  95.9 us (56%)
  waiting for transfers between devices  37.2 us (22%)
  local copies, waits for them, and re-layouts  23.2 us (13%)
  matrix products  5.85 us (3%)
  starting transfers between devices  5 us (3%)
  other arithmetic  4.01 us (2%)
    pallas_call x1, Pallas kernels, share(): pl.pallas_call(functools.partial(share_kernel, count), out_shape=jax.Shap...  56 us
    all_to_all x1, waiting for transfers between devices, body(): lax.all_to_all(vectors.reshape(1, points), 'band', split_axis=1, concat_a...  37.2 us
    pallas_call x1, Pallas kernels, exchange(): pl.pallas_call(functools.partial(exchange_kernel, count), out_shape=(jax....  25.6 us
    pallas_call x1, Pallas kernels, sum_all(): pl.pallas_call(functools.partial(sum_kernel, count), out_shape=jax.ShapeD...  13 us
    all_to_all x1, local copies, waits for them, and re-layouts, body(): lax.all_to_all(vectors.reshape(1, points), 'band', split_axis=1, concat_a...  5.99 us
    unnamed x20, local copies, waits for them, and re-layouts  5.8 us
    all_to_all x1, starting transfers between devices, body(): lax.all_to_all(vectors.reshape(1, points), 'band', split_axis=1, concat_a...  5 us
    reshape x1, local copies, waits for them, and re-layouts, body(): partners.reshape(NP, NG, NG, NG)  4.64 us
  transfers between devices with their start and end apart: 1, of which 1 were waited for; matrix products, arithmetic and copies ran while one was open for 2% of the time, Pallas kernels for 0%

profile of v5, /device:TPU:0, one launch (start us, length us, event | category | flops | bytes accessed | tf_op | source)
XLA Modules:
  0.0 171.4 jit_solution(6389591244394587681)
XLA Ops:
  0.0 0.0 copy-start.1
  0.0 2.2 %copy-done.1 = bf16[4,512000]{1,0:T(4,128)(2,1)S(1)} copy-done((bf16[4,512000]{1,0:T(4,128)(2,1)S(1)}, bf16[4,512000]{1,0:T(4,128)(2,1)}, u32[]{:S(2)}) %copy-start.1) | copy-done | bytes 4096024
  2.2 1.4 pick.1
  3.6 0.0 copy-start.2
  3.6 1.0 copy-done.2
  4.5 1.5 reshape.35.slabs
  6.0 2.6 %reshape.32.target = bf16[80,80,80]{2,1,0:T(8,128)(2,1)} reshape(bf16[4000,128]{1,0:T(8,128)(2,1)S(1)} %get-tuple-element.9) | data formatting | bytes 2048000 | tf_op jit(solution)/shard_map/reshape | solution.py:358
  8.6 0.0 copy-start.3
  8.6 1.2 copy-done.3
  9.9 56.0 %share.1 = bf16[2,4,5,200,128]{4,3,2,1,0:T(8,128)(2,1)S(1)} custom-call(bf16[4,5,200,128]{3,2,1,0:T(8,128)(2,1)S(1)} %bitcast.20), custom_call_target="tpu_custom_call" | custom-call | tf_op jit(solution)/shard_map/share/pallas_call | solution.py:153
  65.8 0.0 copy-start.4
  65.8 0.0 copy-start.5
  65.9 0.0 copy-start.6
  65.9 0.0 copy-start.7
  65.9 0.0 copy-start.8
  65.9 0.0 copy-start.9
  65.9 4.6 %reshape.34.partners = bf16[2,80,80,80]{3,2,1,0:T(8,128)(2,1)} reshape(bf16[2,4,5,200,128]{4,3,2,1,0:T(8,128)(2,1)S(1)} %share.1) | data formatting | bytes 4096000 | tf_op jit(solution)/shard_map/reshape | solution.py:359
  70.6 0.0 copy-done.4
  70.6 0.0 copy-done.5
  70.6 0.0 copy-done.6
  70.6 0.0 copy-done.7
  70.6 0.0 copy-done.8
  70.6 0.0 copy-done.9
  70.6 0.0 copy-start
  70.6 1.4 copy-done
  72.0 25.6 %exchange.1 = (f32[80,80,80]{2,1,0:T(8,128)}, bf16[16,8,4000]{2,1,0:T(8,128)(2,1)S(1)}) custom-call(bf16[80,80,80]{2,1,0:T(8,128)(2,1)S(1)} %copy-done, bf16[2,80,80,80]{3,2,1,0:T(8,128)(2,1)} %reshape.34.partners, bf16[80,240]{1,0:T(8,128)(2,1)S(1)} %copy-done.8, bf16[80,240]{1,0:T(8,128)(2,1)S(1)} %copy-done.7, bf16[80,256]{1,0:T(8,128)(2,1)S(1)} %copy-done.6, ...), custom_call_target="tpu_custom_call" | custom-call | flops 983040000 | bytes 8388608 | tf_op jit(solution)/shard_map/exchange/pallas_call | solution.py:322
  97.6 6.0 %all_to_all.15 = f32[1,16,32000]{2,0,1:T(1,128)} reshape(f32[80,80,80]{2,1,0:T(8,128)} %get-tuple-element.12) | data formatting | bytes 4096000 | tf_op jit(solution)/shard_map/all_to_all | solution.py:363
  103.6 5.0 %all-to-all-start = ((f32[1,16,32000]{2,0,1:T(1,128)}), f32[1,16,32000]{2,0,1:T(1,128)S(1)}, u32[]{:S(2)}, u32[]{:S(2)}) async-start(f32[1,16,32000]{2,0,1:T(1,128)} %all_to_all.15), calls=%async_computation | async-start | bytes 4096000 | tf_op jit(solution)/shard_map/all_to_all | solution.py:363
  108.6 2.6 %reshape.36 = bf16[16,32000]{1,0:T(8,128)(2,1)} reshape(bf16[16,8,4000]{2,1,0:T(8,128)(2,1)S(1)} %get-tuple-element.11) | data formatting | bytes 2048000 | tf_op jit(solution)/shard_map/reshape | solution.py:366
  111.2 37.2 %all-to-all-done = f32[1,16,32000]{2,0,1:T(1,128)S(1)} async-done(((f32[1,16,32000]{2,0,1:T(1,128)}), f32[1,16,32000]{2,0,1:T(1,128)S(1)}, u32[]{:S(2)}, u32[]{:S(2)}) %all-to-all-start) | async-done | bytes 2048032 | tf_op jit(solution)/shard_map/all_to_all | solution.py:363
  148.4 2.7 %fusion.6.part = f32[16,16]{1,0:T(8,128)S(1)} fusion(bf16[16,32000]{1,0:T(8,128)(2,1)} %reshape.36, f32[1,16,32000]{2,0,1:T(1,128)S(1)} %all-to-all-done), kind=kOutput, calls=%fused_computation.6 | convolution fusion | flops 98304256 | bytes 3073024 | tf_op jit(solution)/shard_map/ap,bp->ab/dot_general | solution.py:367
  151.1 13.0 %sum_all.1 = f32[16,16]{1,0:T(8,128)S(1)} custom-call(f32[16,16]{1,0:T(8,128)S(1)} %fusion.6.part), custom_call_target="tpu_custom_call" | custom-call | tf_op jit(solution)/shard_map/sum_all/pallas_call | solution.py:187
  164.1 0.1 copy.10
  164.2 1.5 cholesky.16
  165.7 0.6 compare_reduce_fusion
  166.3 0.6 fusion.9
  167.0 1.2 custom-call.6
  168.2 3.2 %fusion = f32[16,32000]{1,0:T(8,128)} fusion(f32[1,16,32000]{2,0,1:T(1,128)S(1)} %all-to-all-done, f32[1,16,16]{1,2,0:T(8,128)S(1)} %custom-call.6), kind=kOutput, calls=%fused_computation | convolution fusion | flops 98304000 | bytes 4097024 | tf_op jit(solution)/shard_map/jit(_solve_triangular)/triangular_solve | solution.py:371
  (2 shorter events, 0.0 us)
Async XLA Ops:
  0.0 2.2 %copy-start.1 = (bf16[4,512000]{1,0:T(4,128)(2,1)S(1)}, bf16[4,512000]{1,0:T(4,128)(2,1)}, u32[]{:S(2)}) copy-start(bf16[4,512000]{1,0:T(4,128)(2,1)} %orbitals.1) | copy-start | bytes 12288004
  3.6 1.0 copy-start.2
  8.6 1.2 copy-start.3
  65.8 4.7 %copy-start.4 = (f32[80,256]{1,0:T(8,128)S(1)}, f32[80,256]{1,0:T(8,128)}, u32[]{:S(2)}) copy-start(f32[80,256]{1,0:T(8,128)} %constant.50.clone.row_squares) | copy-start | bytes 245764
  65.8 4.7 %copy-start.5 = (bf16[128,256]{1,0:T(8,128)(2,1)S(1)}, bf16[128,256]{1,0:T(8,128)(2,1)}, u32[]{:S(2)}) copy-start(bf16[128,256]{1,0:T(8,128)(2,1)} %constant.49.clone.inverse_right) | copy-start | bytes 196612
  65.9 4.7 %copy-start.6 = (bf16[80,256]{1,0:T(8,128)(2,1)S(1)}, bf16[80,256]{1,0:T(8,128)(2,1)}, u32[]{:S(2)}) copy-start(bf16[80,256]{1,0:T(8,128)(2,1)} %constant.48.clone.forward_right) | copy-start | bytes 122884
  65.9 4.7 %copy-start.7 = (bf16[80,240]{1,0:T(8,128)(2,1)S(1)}, bf16[80,240]{1,0:T(8,128)(2,1)}, u32[]{:S(2)}) copy-start(bf16[80,240]{1,0:T(8,128)(2,1)} %constant.47.clone.inverse_left) | copy-start | bytes 115204
  65.9 4.7 %copy-start.8 = (bf16[80,240]{1,0:T(8,128)(2,1)S(1)}, bf16[80,240]{1,0:T(8,128)(2,1)}, u32[]{:S(2)}) copy-start(bf16[80,240]{1,0:T(8,128)(2,1)} %constant.46.clone.forward_left) | copy-start | bytes 115204
  65.9 4.7 %copy-start.9 = (f32[1,256]{1,0:T(1,128)S(1)}, f32[1,256]{1,0:T(1,128)}, u32[]{:S(2)}) copy-start(f32[1,256]{1,0:T(1,128)} %constant.51.clone.lane_squares) | copy-start | bytes 3076
  70.6 1.4 copy-start
  103.6 44.8 %all-to-all-start = ((f32[1,16,32000]{2,0,1:T(1,128)}), f32[1,16,32000]{2,0,1:T(1,128)S(1)}, u32[]{:S(2)}, u32[]{:S(2)}) async-start(f32[1,16,32000]{2,0,1:T(1,128)} %all_to_all.15), calls=%async_computation | async-start | bytes 4096000 | tf_op jit(solution)/shard_map/all_to_all | solution.py:363

commit v6 on v5

--- a/solution.py
+++ b/solution.py
@@ -153,14 +153,14 @@
     return pl.pallas_call(
         functools.partial(share_kernel, count),
         out_shape=jax.ShapeDtypeStruct((NP,) + row.shape, row.dtype),
-        in_specs=[anywhere],
+        in_specs=[pl.BlockSpec(memory_space=pltpu.HBM)],
         out_specs=anywhere,
         scratch_shapes=[
             dma((QUARTERS - 1, CHUNKS)), dma((NP, planes - 1, CHUNKS)),
             dma((NP, QUARTERS - 1, CHUNKS)), dma((NP, QUARTERS, CHUNKS)), dma,
         ],
         compiler_params=pltpu.CompilerParams(
-            collective_id=0, has_side_effects=True, vmem_limit_bytes=1 << 20
+            collective_id=0, has_side_effects=True, vmem_limit_bytes=60 << 20
         ),
         name="share",
     )(row)
@@ -247,11 +247,17 @@
     return both[:, :PAD] + both[:, PAD:] + dot(low, table[:, :PAD])
 
 
-def exchange_kernel(count, target, partners, forward_left, inverse_left, forward_right,
+def exchange_kernel(count, target_in, partners_in, forward_left, inverse_left, forward_right,
                     inverse_right, row_squares, lane_squares, slabs, vectors, gathered, one, two,
-                    send, receive, own_sem):
+                    target, partners, done, send, receive, own_sem, load_sem, done_sem):
     group = 8
     me = lax.axis_index("band")
+    loads = [
+        pltpu.make_async_copy(target_in, target, load_sem.at[0]),
+        pltpu.make_async_copy(partners_in, partners, load_sem.at[1]),
+    ]
+    for load in loads:
+        load.start()
     barrier_all(me, count)
 
     def slab(step):
@@ -262,6 +268,8 @@
         slab(step).start()
     own = pltpu.make_async_copy(slabs.at[me], gathered.at[me], own_sem)
     own.start()
+    for load in loads:
+        load.wait()
 
     def ahead(step, carry):
         planes = pl.ds(step * group, group)
@@ -303,10 +311,17 @@
             potential = from_right(values[:, r * PAD : (r + 1) * PAD], inverse_right[...])
             potential = potential.reshape(group, NG, PAD)[:, :, :NG]
             total -= partners[r, planes].astype(jnp.float32) * potential
-        vectors[planes] = total
+        done[planes] = total
+        stored(step).start()
         return carry
 
+    def stored(step):
+        planes = pl.ds(step * group, group)
+        return pltpu.make_async_copy(done.at[planes], vectors.at[planes], done_sem.at[step])
+
     lax.fori_loop(0, NG // group, back, 0)
+    for step in range(NG // group):
+        stored(step).wait()
     own.wait()
     for step in range(1, count):
         slab(step).wait()
@@ -325,12 +340,17 @@
             jax.ShapeDtypeStruct((NG, NG, NG), jnp.float32),
             jax.ShapeDtypeStruct(slabs.shape, slabs.dtype),
         ),
-        in_specs=[vmem] * 8 + [anywhere],
-        out_specs=(vmem, anywhere),
+        in_specs=[anywhere] * 2 + [vmem] * 6 + [anywhere],
+        out_specs=(anywhere, anywhere),
         scratch_shapes=[pltpu.VMEM((NG, NG, NP * PAD), jnp.float32)] * 2
-        + [dma((count,)), dma((count,)), dma],
+        + [
+            pltpu.VMEM(target.shape, target.dtype),
+            pltpu.VMEM(partners.shape, partners.dtype),
+            pltpu.VMEM((NG, NG, NG), jnp.float32),
+            dma((count,)), dma((count,)), dma, dma((2,)), dma((NG // 8,)),
+        ],
         compiler_params=pltpu.CompilerParams(
-            collective_id=2, has_side_effects=True, vmem_limit_bytes=48 << 20
+            collective_id=2, has_side_effects=True, vmem_limit_bytes=60 << 20
         ),
         cost_estimate=pl.CostEstimate(
             flops=12 * NP * NG**4, bytes_accessed=8 << 20, transcendentals=0

time: 172 us -> 194 us (1.13)
  Pallas kernels: 95.9 us -> 124 us
  waiting for transfers between devices: 37.2 us -> 34 us
    pallas_call x1, Pallas kernels: 56 us -> 86.1 us  [share(): pl.pallas_call(functools.partial(share_kernel, count), out_shape=jax.Shap...]
    all_to_all x1, waiting for transfers between devices: 37.2 us -> 34 us  [body(): lax.all_to_all(vectors.reshape(1, points), 'band', split_axis=1, concat_a...]
    pallas_call x1, Pallas kernels: 13 us -> 10.3 us  [sum_all(): pl.pallas_call(functools.partial(sum_kernel, count), out_shape=jax.ShapeD...]
    unnamed x20 -> x4, local copies, waits for them, and re-layouts: 5.8 us -> 3.16 us
  transfers between devices with their start and end apart: 1 -> 1, of which waited for: 1 -> 1; matrix products, arithmetic and copies ran while one was open for 2% -> 1% of each run, Pallas kernels for 0% -> 0%
where the time goes in v6:
time: 194 us
  Pallas kernels  124 us (64%)
  waiting for transfers between devices  34 us (18%)
  local copies, waits for them, and re-layouts  23.5 us (12%)
  matrix products  4.64 us (2%)
  other arithmetic  4.01 us (2%)
  starting transfers between devices  3.92 us (2%)
    pallas_call x1, Pallas kernels, share(): pl.pallas_call(functools.partial(share_kernel, count), out_shape=jax.Shap...  86.1 us
    all_to_all x1, waiting for transfers between devices, body(): lax.all_to_all(vectors.reshape(1, points), 'band', split_axis=1, concat_a...  34 us
    pallas_call x1, Pallas kernels, exchange(): pl.pallas_call(functools.partial(exchange_kernel, count), out_shape=(jax....  25.9 us
    pallas_call x1, Pallas kernels, sum_all(): pl.pallas_call(functools.partial(sum_kernel, count), out_shape=jax.ShapeD...  10.3 us
    reshape x1, local copies, waits for them, and re-layouts, body(): partners.reshape(NP, NG, NG, NG)  6.37 us
    all_to_all x1, local copies, waits for them, and re-layouts, body(): lax.all_to_all(vectors.reshape(1, points), 'band', split_axis=1, concat_a...  5.99 us
    all_to_all x1, starting transfers between devices, body(): lax.all_to_all(vectors.reshape(1, points), 'band', split_axis=1, concat_a...  3.92 us
  transfers between devices with their start and end apart: 1, of which 1 were waited for; matrix products, arithmetic and copies ran while one was open for 1% of the time, Pallas kernels for 0%

profile of v6, /device:TPU:0, one launch (start us, length us, event | category | flops | bytes accessed | tf_op | source)
XLA Modules:
  0.0 193.8 jit_solution(371291303912075341)
XLA Ops:
  0.0 0.0 copy-start
  0.0 2.2 %copy-done = bf16[4,512000]{1,0:T(4,128)(2,1)S(1)} copy-done((bf16[4,512000]{1,0:T(4,128)(2,1)S(1)}, bf16[4,512000]{1,0:T(4,128)(2,1)}, u32[]{:S(2)}) %copy-start) | copy-done | bytes 4096024
  2.2 1.4 pick.1
  3.6 0.0 copy-start.1
  3.6 1.0 copy-done.1
  4.6 2.5 %reshape.35.slabs = bf16[16,8,4000]{2,1,0:T(8,128)(2,1)} reshape(bf16[4000,128]{1,0:T(8,128)(2,1)S(1)} %get-tuple-element.9) | data formatting | bytes 2048000 | tf_op jit(solution)/shard_map/reshape | solution.py:380
  7.0 2.6 %reshape.32.target_in = bf16[80,80,80]{2,1,0:T(8,128)(2,1)} reshape(bf16[4000,128]{1,0:T(8,128)(2,1)S(1)} %get-tuple-element.9) | data formatting | bytes 2048000 | tf_op jit(solution)/shard_map/reshape | solution.py:378
  9.7 86.1 %share.1 = bf16[2,4,5,200,128]{4,3,2,1,0:T(8,128)(2,1)} custom-call(bf16[4,5,200,128]{3,2,1,0:T(8,128)(2,1)} %bitcast.20), custom_call_target="tpu_custom_call" | custom-call | tf_op jit(solution)/shard_map/share/pallas_call | solution.py:153
  95.7 6.4 %reshape.34.partners_in = bf16[2,80,80,80]{3,2,1,0:T(8,128)(2,1)} reshape(bf16[2,4,5,200,128]{4,3,2,1,0:T(8,128)(2,1)} %share.1) | data formatting | bytes 4096000 | tf_op jit(solution)/shard_map/reshape | solution.py:379
  102.1 25.9 %exchange.1 = (f32[80,80,80]{2,1,0:T(8,128)}, bf16[16,8,4000]{2,1,0:T(8,128)(2,1)}) custom-call(bf16[80,80,80]{2,1,0:T(8,128)(2,1)} %reshape.32.target_in, bf16[2,80,80,80]{3,2,1,0:T(8,128)(2,1)} %reshape.34.partners_in, bf16[80,240]{1,0:T(8,128)(2,1)} %constant.46.clone.forward_left, bf16[80,240]{1,0:T(8,128)(2,1)} %constant.47.clone.inverse_left, ...), custom_call_target="tpu_custom_call" | custom-call | flops 983040000 | bytes 8388608 | tf_op jit(solution)/shard_map/exchange/pallas_call | solution.py:337
  128.0 6.0 %all_to_all.15 = f32[1,16,32000]{2,0,1:T(1,128)} reshape(f32[80,80,80]{2,1,0:T(8,128)} %get-tuple-element.12) | data formatting | bytes 4096000 | tf_op jit(solution)/shard_map/all_to_all | solution.py:383
  134.0 3.9 %all-to-all-start = ((f32[1,16,32000]{2,0,1:T(1,128)}), f32[1,16,32000]{2,0,1:T(1,128)S(1)}, u32[]{:S(2)}, u32[]{:S(2)}) async-start(f32[1,16,32000]{2,0,1:T(1,128)} %all_to_all.15), calls=%async_computation | async-start | bytes 4096000 | tf_op jit(solution)/shard_map/all_to_all | solution.py:383
  137.9 2.8 %reshape.36 = bf16[16,32000]{1,0:T(8,128)(2,1)S(1)} reshape(bf16[16,8,4000]{2,1,0:T(8,128)(2,1)} %get-tuple-element.11) | data formatting | bytes 2048000 | tf_op jit(solution)/shard_map/reshape | solution.py:386
  140.7 34.0 %all-to-all-done = f32[1,16,32000]{2,0,1:T(1,128)S(1)} async-done(((f32[1,16,32000]{2,0,1:T(1,128)}), f32[1,16,32000]{2,0,1:T(1,128)S(1)}, u32[]{:S(2)}, u32[]{:S(2)}) %all-to-all-start) | async-done | bytes 2048032 | tf_op jit(solution)/shard_map/all_to_all | solution.py:383
  174.8 1.5 fusion.6.part
  176.2 10.3 %sum_all.1 = f32[16,16]{1,0:T(8,128)S(1)} custom-call(f32[16,16]{1,0:T(8,128)S(1)} %fusion.6.part), custom_call_target="tpu_custom_call" | custom-call | tf_op jit(solution)/shard_map/sum_all/pallas_call | solution.py:187
  186.5 0.1 copy.10
  186.6 1.5 cholesky.16
  188.1 0.6 compare_reduce_fusion
  188.7 0.6 fusion.9
  189.4 1.2 custom-call.6
  190.6 3.2 %fusion = f32[16,32000]{1,0:T(8,128)} fusion(f32[1,16,32000]{2,0,1:T(1,128)S(1)} %all-to-all-done, f32[1,16,16]{1,2,0:T(8,128)S(1)} %custom-call.6), kind=kOutput, calls=%fused_computation | convolution fusion | flops 98304000 | bytes 4097024 | tf_op jit(solution)/shard_map/jit(_solve_triangular)/triangular_solve | solution.py:391
  (2 shorter events, 0.0 us)
Async XLA Ops:
  0.0 2.2 %copy-start = (bf16[4,512000]{1,0:T(4,128)(2,1)S(1)}, bf16[4,512000]{1,0:T(4,128)(2,1)}, u32[]{:S(2)}) copy-start(bf16[4,512000]{1,0:T(4,128)(2,1)} %orbitals.1) | copy-start | bytes 12288004
  3.6 1.0 copy-start.1
  134.0 40.8 %all-to-all-start = ((f32[1,16,32000]{2,0,1:T(1,128)}), f32[1,16,32000]{2,0,1:T(1,128)S(1)}, u32[]{:S(2)}, u32[]{:S(2)}) async-start(f32[1,16,32000]{2,0,1:T(1,128)} %all_to_all.15), calls=%async_computation | async-start | bytes 4096000 | tf_op jit(solution)/shard_map/all_to_all | solution.py:383

commit v7 on v6

--- a/solution.py
+++ b/solution.py
@@ -160,7 +160,7 @@
             dma((NP, QUARTERS - 1, CHUNKS)), dma((NP, QUARTERS, CHUNKS)), dma,
         ],
         compiler_params=pltpu.CompilerParams(
-            collective_id=0, has_side_effects=True, vmem_limit_bytes=60 << 20
+            collective_id=0, has_side_effects=True, vmem_limit_bytes=1 << 20
         ),
         name="share",
     )(row)

time: 194 us -> 165 us (0.85)
  Pallas kernels: 124 us -> 94.4 us
  local copies, waits for them, and re-layouts: 23.5 us -> 20.8 us
  waiting for transfers between devices: 34 us -> 36.6 us
    pallas_call x1, Pallas kernels: 86.1 us -> 56 us  [share(): pl.pallas_call(functools.partial(share_kernel, count), out_shape=jax.Shap...]
    pallas_call x1, Pallas kernels: 10.3 us -> 13 us  [sum_all(): pl.pallas_call(functools.partial(sum_kernel, count), out_shape=jax.ShapeD...]
    all_to_all x1, waiting for transfers between devices: 34 us -> 36.6 us  [body(): lax.all_to_all(vectors.reshape(1, points), 'band', split_axis=1, concat_a...]
  transfers between devices with their start and end apart: 1 -> 1, of which waited for: 1 -> 1; matrix products, arithmetic and copies ran while one was open for 1% -> 2% of each run, Pallas kernels for 0% -> 0%
where the time goes in v7:
time: 165 us
  Pallas kernels  94.4 us (57%)
  waiting for transfers between devices  36.6 us (22%)
  local copies, waits for them, and re-layouts  20.8 us (13%)
  matrix products  4.64 us (3%)
  starting transfers between devices  4.61 us (3%)
  other arithmetic  4.01 us (2%)
    pallas_call x1, Pallas kernels, share(): pl.pallas_call(functools.partial(share_kernel, count), out_shape=jax.Shap...  56 us
    all_to_all x1, waiting for transfers between devices, body(): lax.all_to_all(vectors.reshape(1, points), 'band', split_axis=1, concat_a...  36.6 us
    pallas_call x1, Pallas kernels, exchange(): pl.pallas_call(functools.partial(exchange_kernel, count), out_shape=(jax....  24.1 us
    pallas_call x1, Pallas kernels, sum_all(): pl.pallas_call(functools.partial(sum_kernel, count), out_shape=jax.ShapeD...  13 us
    all_to_all x1, local copies, waits for them, and re-layouts, body(): lax.all_to_all(vectors.reshape(1, points), 'band', split_axis=1, concat_a...  5.99 us
    reshape x1, local copies, waits for them, and re-layouts, body(): partners.reshape(NP, NG, NG, NG)  4.63 us
    all_to_all x1, starting transfers between devices, body(): lax.all_to_all(vectors.reshape(1, points), 'band', split_axis=1, concat_a...  4.61 us
  transfers between devices with their start and end apart: 1, of which 1 were waited for; matrix products, arithmetic and copies ran while one was open for 2% of the time, Pallas kernels for 0%

profile of v7, /device:TPU:0, one launch (start us, length us, event | category | flops | bytes accessed | tf_op | source)
XLA Modules:
  0.0 165.2 jit_solution(14499627917309550848)
XLA Ops:
  0.0 0.0 copy-start
  0.0 2.2 %copy-done = bf16[4,512000]{1,0:T(4,128)(2,1)S(1)} copy-done((bf16[4,512000]{1,0:T(4,128)(2,1)S(1)}, bf16[4,512000]{1,0:T(4,128)(2,1)}, u32[]{:S(2)}) %copy-start) | copy-done | bytes 4096024
  2.2 1.4 pick.1
  3.6 2.5 %reshape.35.slabs = bf16[16,8,4000]{2,1,0:T(8,128)(2,1)} reshape(bf16[4000,128]{1,0:T(8,128)(2,1)S(1)} %get-tuple-element.9) | data formatting | bytes 2048000 | tf_op jit(solution)/shard_map/reshape | solution.py:380
  6.1 2.6 %reshape.32.target_in = bf16[80,80,80]{2,1,0:T(8,128)(2,1)} reshape(bf16[4000,128]{1,0:T(8,128)(2,1)S(1)} %get-tuple-element.9) | data formatting | bytes 2048000 | tf_op jit(solution)/shard_map/reshape | solution.py:378
  8.7 56.0 %share.1 = bf16[2,4,5,200,128]{4,3,2,1,0:T(8,128)(2,1)S(1)} custom-call(bf16[4,5,200,128]{3,2,1,0:T(8,128)(2,1)S(1)} %bitcast.20), custom_call_target="tpu_custom_call" | custom-call | tf_op jit(solution)/shard_map/share/pallas_call | solution.py:153
  64.7 4.6 %reshape.34.partners_in = bf16[2,80,80,80]{3,2,1,0:T(8,128)(2,1)} reshape(bf16[2,4,5,200,128]{4,3,2,1,0:T(8,128)(2,1)S(1)} %share.1) | data formatting | bytes 4096000 | tf_op jit(solution)/shard_map/reshape | solution.py:379
  69.3 24.1 %exchange.1 = (f32[80,80,80]{2,1,0:T(8,128)}, bf16[16,8,4000]{2,1,0:T(8,128)(2,1)}) custom-call(bf16[80,80,80]{2,1,0:T(8,128)(2,1)} %reshape.32.target_in, bf16[2,80,80,80]{3,2,1,0:T(8,128)(2,1)} %reshape.34.partners_in, bf16[80,240]{1,0:T(8,128)(2,1)} %constant.46.clone.forward_left, bf16[80,240]{1,0:T(8,128)(2,1)} %constant.47.clone.inverse_left, ...), custom_call_target="tpu_custom_call" | custom-call | flops 983040000 | bytes 8388608 | tf_op jit(solution)/shard_map/exchange/pallas_call | solution.py:337
  93.4 6.0 %all_to_all.15 = f32[1,16,32000]{2,0,1:T(1,128)} reshape(f32[80,80,80]{2,1,0:T(8,128)} %get-tuple-element.12) | data formatting | bytes 4096000 | tf_op jit(solution)/shard_map/all_to_all | solution.py:383
  99.4 4.6 %all-to-all-start = ((f32[1,16,32000]{2,0,1:T(1,128)}), f32[1,16,32000]{2,0,1:T(1,128)S(1)}, u32[]{:S(2)}, u32[]{:S(2)}) async-start(f32[1,16,32000]{2,0,1:T(1,128)} %all_to_all.15), calls=%async_computation | async-start | bytes 4096000 | tf_op jit(solution)/shard_map/all_to_all | solution.py:383
  104.0 2.8 %reshape.36 = bf16[16,32000]{1,0:T(8,128)(2,1)S(1)} reshape(bf16[16,8,4000]{2,1,0:T(8,128)(2,1)} %get-tuple-element.11) | data formatting | bytes 2048000 | tf_op jit(solution)/shard_map/reshape | solution.py:386
  106.8 36.6 %all-to-all-done = f32[1,16,32000]{2,0,1:T(1,128)S(1)} async-done(((f32[1,16,32000]{2,0,1:T(1,128)}), f32[1,16,32000]{2,0,1:T(1,128)S(1)}, u32[]{:S(2)}, u32[]{:S(2)}) %all-to-all-start) | async-done | bytes 2048032 | tf_op jit(solution)/shard_map/all_to_all | solution.py:383
  143.4 1.5 fusion.6.part
  144.9 13.0 %sum_all.1 = f32[16,16]{1,0:T(8,128)S(1)} custom-call(f32[16,16]{1,0:T(8,128)S(1)} %fusion.6.part), custom_call_target="tpu_custom_call" | custom-call | tf_op jit(solution)/shard_map/sum_all/pallas_call | solution.py:187
  157.9 0.1 copy.10
  158.0 1.5 cholesky.16
  159.4 0.6 compare_reduce_fusion
  160.1 0.6 fusion.9
  160.7 1.2 custom-call.6
  162.0 3.2 %fusion = f32[16,32000]{1,0:T(8,128)} fusion(f32[1,16,32000]{2,0,1:T(1,128)S(1)} %all-to-all-done, f32[1,16,16]{1,2,0:T(8,128)S(1)} %custom-call.6), kind=kOutput, calls=%fused_computation | convolution fusion | flops 98304000 | bytes 4097024 | tf_op jit(solution)/shard_map/jit(_solve_triangular)/triangular_solve | solution.py:391
  (2 shorter events, 0.0 us)
Async XLA Ops:
  0.0 2.2 %copy-start = (bf16[4,512000]{1,0:T(4,128)(2,1)S(1)}, bf16[4,512000]{1,0:T(4,128)(2,1)}, u32[]{:S(2)}) copy-start(bf16[4,512000]{1,0:T(4,128)(2,1)} %orbitals.1) | copy-start | bytes 12288004
  99.4 44.1 %all-to-all-start = ((f32[1,16,32000]{2,0,1:T(1,128)}), f32[1,16,32000]{2,0,1:T(1,128)S(1)}, u32[]{:S(2)}, u32[]{:S(2)}) async-start(f32[1,16,32000]{2,0,1:T(1,128)} %all_to_all.15), calls=%async_computation | async-start | bytes 4096000 | tf_op jit(solution)/shard_map/all_to_all | solution.py:383

commit v8 on v7

--- a/solution.py
+++ b/solution.py
@@ -97,9 +97,6 @@
     for r in range(NP):
         @pl.when(me == r * stride)
         def _():
-            for c in range(CHUNKS):
-                for q in range(1, QUARTERS):
-                    first(r, q, c).start()
             own = pltpu.make_async_copy(row, partners.at[r], own_sem)
             own.start()
             own.wait()
@@ -109,6 +106,11 @@
             @pl.when(me != r * stride)
             def _():
                 arrived(r, column, c)
+
+            @pl.when(me == r * stride)
+            def _():
+                for q in range(1, QUARTERS):
+                    first(r, q, c).start()
 
             @pl.when(plane == r * stride // QUARTERS)
             def _():

time: 165 us -> 165 us (level)
    pallas_call x1, Pallas kernels: 56 us -> 59.2 us  [share(): pl.pallas_call(functools.partial(share_kernel, count), out_shape=jax.Shap...]
    pallas_call x1, Pallas kernels: 13 us -> 10.9 us  [sum_all(): pl.pallas_call(functools.partial(sum_kernel, count), out_shape=jax.ShapeD...]
where the time goes in v8:
time: 165 us
  Pallas kernels  95.6 us (58%)
  waiting for transfers between devices  35.1 us (21%)
  local copies, waits for them, and re-layouts  20.8 us (13%)
  matrix products  4.64 us (3%)
  starting transfers between devices  4.62 us (3%)
  other arithmetic  4.01 us (2%)
    pallas_call x1, Pallas kernels, share(): pl.pallas_call(functools.partial(share_kernel, count), out_shape=jax.Shap...  59.2 us
    all_to_all x1, waiting for transfers between devices, body(): lax.all_to_all(vectors.reshape(1, points), 'band', split_axis=1, concat_a...  35.1 us
    pallas_call x1, Pallas kernels, exchange(): pl.pallas_call(functools.partial(exchange_kernel, count), out_shape=(jax....  24.1 us
    pallas_call x1, Pallas kernels, sum_all(): pl.pallas_call(functools.partial(sum_kernel, count), out_shape=jax.ShapeD...  10.9 us
    all_to_all x1, local copies, waits for them, and re-layouts, body(): lax.all_to_all(vectors.reshape(1, points), 'band', split_axis=1, concat_a...  5.99 us
    reshape x1, local copies, waits for them, and re-layouts, body(): partners.reshape(NP, NG, NG, NG)  4.63 us
    all_to_all x1, starting transfers between devices, body(): lax.all_to_all(vectors.reshape(1, points), 'band', split_axis=1, concat_a...  4.62 us
  transfers between devices with their start and end apart: 1, of which 1 were waited for; matrix products, arithmetic and copies ran while one was open for 2% of the time, Pallas kernels for 0%

profile of v8, /device:TPU:0, one launch (start us, length us, event | category | flops | bytes accessed | tf_op | source)
XLA Modules:
  0.0 164.8 jit_solution(2578982054768220241)
XLA Ops:
  0.0 0.0 copy-start
  0.0 2.2 %copy-done = bf16[4,512000]{1,0:T(4,128)(2,1)S(1)} copy-done((bf16[4,512000]{1,0:T(4,128)(2,1)S(1)}, bf16[4,512000]{1,0:T(4,128)(2,1)}, u32[]{:S(2)}) %copy-start) | copy-done | bytes 4096024
  2.2 1.4 pick.1
  3.6 2.5 %reshape.35.slabs = bf16[16,8,4000]{2,1,0:T(8,128)(2,1)} reshape(bf16[4000,128]{1,0:T(8,128)(2,1)S(1)} %get-tuple-element.9) | data formatting | bytes 2048000 | tf_op jit(solution)/shard_map/reshape | solution.py:382
  6.1 2.6 %reshape.32.target_in = bf16[80,80,80]{2,1,0:T(8,128)(2,1)} reshape(bf16[4000,128]{1,0:T(8,128)(2,1)S(1)} %get-tuple-element.9) | data formatting | bytes 2048000 | tf_op jit(solution)/shard_map/reshape | solution.py:380
  8.7 59.2 %share.1 = bf16[2,4,5,200,128]{4,3,2,1,0:T(8,128)(2,1)S(1)} custom-call(bf16[4,5,200,128]{3,2,1,0:T(8,128)(2,1)S(1)} %bitcast.20), custom_call_target="tpu_custom_call" | custom-call | tf_op jit(solution)/shard_map/share/pallas_call | solution.py:155
  67.9 4.6 %reshape.34.partners_in = bf16[2,80,80,80]{3,2,1,0:T(8,128)(2,1)} reshape(bf16[2,4,5,200,128]{4,3,2,1,0:T(8,128)(2,1)S(1)} %share.1) | data formatting | bytes 4096000 | tf_op jit(solution)/shard_map/reshape | solution.py:381
  72.5 24.1 %exchange.1 = (f32[80,80,80]{2,1,0:T(8,128)}, bf16[16,8,4000]{2,1,0:T(8,128)(2,1)}) custom-call(bf16[80,80,80]{2,1,0:T(8,128)(2,1)} %reshape.32.target_in, bf16[2,80,80,80]{3,2,1,0:T(8,128)(2,1)} %reshape.34.partners_in, bf16[80,240]{1,0:T(8,128)(2,1)} %constant.46.clone.forward_left, bf16[80,240]{1,0:T(8,128)(2,1)} %constant.47.clone.inverse_left, ...), custom_call_target="tpu_custom_call" | custom-call | flops 983040000 | bytes 8388608 | tf_op jit(solution)/shard_map/exchange/pallas_call | solution.py:339
  96.6 6.0 %all_to_all.15 = f32[1,16,32000]{2,0,1:T(1,128)} reshape(f32[80,80,80]{2,1,0:T(8,128)} %get-tuple-element.12) | data formatting | bytes 4096000 | tf_op jit(solution)/shard_map/all_to_all | solution.py:385
  102.6 4.6 %all-to-all-start = ((f32[1,16,32000]{2,0,1:T(1,128)}), f32[1,16,32000]{2,0,1:T(1,128)S(1)}, u32[]{:S(2)}, u32[]{:S(2)}) async-start(f32[1,16,32000]{2,0,1:T(1,128)} %all_to_all.15), calls=%async_computation | async-start | bytes 4096000 | tf_op jit(solution)/shard_map/all_to_all | solution.py:385
  107.2 2.8 %reshape.36 = bf16[16,32000]{1,0:T(8,128)(2,1)S(1)} reshape(bf16[16,8,4000]{2,1,0:T(8,128)(2,1)} %get-tuple-element.11) | data formatting | bytes 2048000 | tf_op jit(solution)/shard_map/reshape | solution.py:388
  110.0 35.1 %all-to-all-done = f32[1,16,32000]{2,0,1:T(1,128)S(1)} async-done(((f32[1,16,32000]{2,0,1:T(1,128)}), f32[1,16,32000]{2,0,1:T(1,128)S(1)}, u32[]{:S(2)}, u32[]{:S(2)}) %all-to-all-start) | async-done | bytes 2048032 | tf_op jit(solution)/shard_map/all_to_all | solution.py:385
  145.2 1.5 fusion.6.part
  146.6 10.9 %sum_all.1 = f32[16,16]{1,0:T(8,128)S(1)} custom-call(f32[16,16]{1,0:T(8,128)S(1)} %fusion.6.part), custom_call_target="tpu_custom_call" | custom-call | tf_op jit(solution)/shard_map/sum_all/pallas_call | solution.py:189
  157.5 0.1 copy.10
  157.6 1.5 cholesky.16
  159.1 0.6 compare_reduce_fusion
  159.7 0.6 fusion.9
  160.4 1.2 custom-call.6
  161.6 3.2 %fusion = f32[16,32000]{1,0:T(8,128)} fusion(f32[1,16,32000]{2,0,1:T(1,128)S(1)} %all-to-all-done, f32[1,16,16]{1,2,0:T(8,128)S(1)} %custom-call.6), kind=kOutput, calls=%fused_computation | convolution fusion | flops 98304000 | bytes 4097024 | tf_op jit(solution)/shard_map/jit(_solve_triangular)/triangular_solve | solution.py:393
  (2 shorter events, 0.0 us)
Async XLA Ops:
  0.0 2.2 %copy-start = (bf16[4,512000]{1,0:T(4,128)(2,1)S(1)}, bf16[4,512000]{1,0:T(4,128)(2,1)}, u32[]{:S(2)}) copy-start(bf16[4,512000]{1,0:T(4,128)(2,1)} %orbitals.1) | copy-start | bytes 12288004
  102.6 42.6 %all-to-all-start = ((f32[1,16,32000]{2,0,1:T(1,128)}), f32[1,16,32000]{2,0,1:T(1,128)S(1)}, u32[]{:S(2)}, u32[]{:S(2)}) async-start(f32[1,16,32000]{2,0,1:T(1,128)} %all_to_all.15), calls=%async_computation | async-start | bytes 4096000 | tf_op jit(solution)/shard_map/all_to_all | solution.py:385
